TPU v7x, 256 devices: a whole 4x4x8 slice. The times are simulated.
256 devices in a mesh: tm: 8 (over z_lo, y), space: 32 (over z_hi, x, core).
Axes of the slice: x: 4, y: 4, z: 8 (z_hi: 4, z_lo: 2; z = z_hi * 2 + z_lo), core: 2. Of those that a mesh axis runs over, the one named last changes fastest.
Arguments:
- control: float32 [256, 51200], P(('tm', 'space')), may hold values from -4 to 4
- spectrum: float32 [51200], replicated, may hold values from 0.2 to 2
- perturb: bfloat16 [16, 256, 4, 51200], P('tm', None, None, 'space'), may hold values from -0.375 to 0.375
- obs_index: int32 [16, 65536], P('tm', 'space'), may hold values from 0 to 6399
- innovation: float32 [16, 65536], P('tm', 'space'), may hold values from -10 to 10
- obs_sigma: float32 [16, 65536], P('tm', 'space'), may hold values from 0.5 to 2
- qc_class: int32 [16, 65536], P('tm', 'space'), may hold values from 0 to 2
Outputs:
- control_out: float32 [256, 51200], P(('tm', 'space'))
- cost_list: float32 [1], replicated
Inputs may be any that keep to these rules, and one draw needn't show every extreme that they name: `obs_index`: observation o of block o // 2048 observes the cell level * 1600 + point, the point counted within the block's piece of the grid; repeats may occur.
All inputs are finite; a program needn't handle non-finite values.
Results may differ from a plain program's by a relative error of at most 0.0034.
Values may be sent and summed in bfloat16 or wider, within the bound.
No kernel may reach another device: no remote copies, remote signals or barrier semaphores. Data moves between devices by JAX's collectives and lax.ppermute only.
A program may use at most 128 MiB of HBM per device.

v0:
```python
import jax
import jax.numpy as jnp
from jax import lax
from jax.sharding import Mesh
from jax.sharding import PartitionSpec as P

GX = 320
GY = 160
SPACE = ("space_0", "space_1", "space_2")
TM = ("tm_0", "tm_1")
TM_SPACE = ("tm_0", "tm_1", "space_0", "space_1", "space_2")


def joined_along(tiles, dim):
    lengths = list(tiles.shape[1:])
    lengths[dim] *= tiles.shape[0]
    return jnp.moveaxis(tiles, 0, dim).reshape(lengths)


def from_everyone(value, axis):
    copies = jnp.broadcast_to(value, (lax.axis_size(axis), *value.shape))
    return lax.all_to_all(copies, axis, split_axis=0, concat_axis=0, tiled=True)


def gather_directly(value, axis, dim):
    return joined_along(from_everyone(value, axis), dim)


def cut_along(value, dim, count):
    lengths = value.shape
    tiles = value.reshape(*lengths[:dim], count, lengths[dim] // count, *lengths[dim + 1 :])
    return jnp.moveaxis(tiles, dim, 0)


def sent_and_summed(value, axis, dim):
    tiles = cut_along(value, dim, lax.axis_size(axis))
    arrived = lax.all_to_all(tiles, axis, split_axis=0, concat_axis=0, tiled=True)
    return arrived.astype(jnp.float32).sum(axis=0)


def by_axis(value, axes):
    for axis in axes:
        value = lax.psum(value, axis)
    return value


def lookup_tables(segment_length):
    wave_num = jnp.arange(segment_length, dtype=jnp.float32)[:, None]
    grid_positions = jnp.arange(segment_length, dtype=jnp.float32)[None, :]
    basis = jnp.cos(jnp.pi * (grid_positions + 0.5) * wave_num / segment_length) * jnp.sqrt(
        2.0 / segment_length
    )
    return jnp.where(wave_num == 0, basis * jnp.sqrt(0.5), basis)


def synthesize(control, spectrum, basis_x, basis_y):
    coeffs = (control * spectrum[None, :]).reshape(control.shape[0], GX, GY)
    middle = jnp.einsum("kn,mkl->mnl", basis_x, coeffs, precision=lax.Precision.HIGHEST)
    result = jnp.einsum("mnl,lp->mnp", middle, basis_y, precision=lax.Precision.HIGHEST)
    return result.reshape(control.shape[0], GX * GY)


def analyze(adjoint, spectrum, basis_x, basis_y):
    state_fields = adjoint.reshape(adjoint.shape[0], GX, GY)
    middle = jnp.einsum("kn,mnp->mkp", basis_x, state_fields, precision=lax.Precision.HIGHEST)
    result = jnp.einsum("mkp,lp->mkl", middle, basis_y, precision=lax.Precision.HIGHEST)
    return result.reshape(adjoint.shape[0], GX * GY) * spectrum[None, :]


def per_device(control, spectrum, perturb, obs_index, innovation, obs_sigma, qc_class):
    basis_x = lookup_tables(GX)
    basis_y = lookup_tables(GY)
    slot_count = perturb.shape[0]
    levels = perturb.shape[2]
    piece_len = perturb.shape[3]
    radius = jnp.where(qc_class == 0, 4.0, jnp.where(qc_class == 1, 2.0, 1.0)).astype(jnp.float32)

    def scatter_cells(indices, values):
        return jnp.zeros((levels * piece_len,), jnp.float32).at[indices].add(values)

    member_field = synthesize(control, spectrum, basis_x, basis_y).astype(jnp.bfloat16)
    pieces = lax.all_to_all(member_field, SPACE, split_axis=1, concat_axis=0, tiled=True)
    selected_entries = perturb
    increment = jnp.einsum(
        "dzab,zb->dab",
        selected_entries,
        gather_directly(pieces, TM, 0),
        preferred_element_type=jnp.float32,
    )
    cells_flat = increment.reshape(slot_count, levels * piece_len)
    modelled = jnp.take_along_axis(cells_flat, obs_index, axis=1)
    scaled = (modelled - innovation) / obs_sigma
    scaled_sq = scaled * scaled / (radius * radius)
    obs_part = jnp.sum(0.5 * radius * radius * jnp.log1p(scaled_sq))
    back_part = 0.5 * jnp.sum(control * control)
    obs_grad = scaled / ((1.0 + scaled_sq) * obs_sigma)
    control_update = jax.vmap(scatter_cells)(obs_index, obs_grad).astype(jnp.bfloat16)
    control_update = control_update.reshape(slot_count, levels, piece_len)
    selected_entries = perturb
    summed_rows = sent_and_summed(
        jnp.einsum(
            "qiyr,qyr->ir", selected_entries, control_update, preferred_element_type=jnp.float32
        ).astype(jnp.bfloat16),
        TM,
        0,
    )
    adjoint = lax.all_to_all(
        summed_rows.astype(jnp.bfloat16), SPACE, split_axis=0, concat_axis=1, tiled=True
    ).astype(summed_rows.dtype)
    gradient = control + analyze(adjoint, spectrum, basis_x, basis_y)
    grad_part = jnp.sum(gradient * gradient)
    obs_cost = by_axis(obs_part, TM_SPACE)
    back_cost = by_axis(back_part, TM_SPACE)
    grad_sq = by_axis(grad_part, TM_SPACE)
    total_cost = back_cost + obs_cost
    step_size = 0.5 * total_cost / (grad_sq + 1e-06)
    control = control - step_size * gradient
    cost_list = [total_cost]
    return (control, jnp.stack(cost_list))


def solution(mesh):
    split = Mesh(
        mesh.devices.reshape(2, 4, 4, 4, 2), ("tm_0", "tm_1", "space_0", "space_1", "space_2")
    )
    return jax.shard_map(
        per_device,
        mesh=split,
        in_specs=(
            P(TM_SPACE, None),
            P(),
            P(TM, None, None, SPACE),
            P(TM, SPACE),
            P(TM, SPACE),
            P(TM, SPACE),
            P(TM, SPACE),
        ),
        out_specs=(P(TM_SPACE, None), P()),
        check_vma=False,
    )
```

profile of v0, /device:TPU:1, one launch (start us, length us, event | category | flops | bytes accessed | tf_op | source)
XLA Modules:
  0.0 200.4 jit_solution(14478216009850965294)
XLA Ops:
  0.7 2.4 %multiply_reduce_fusion.4 = (f32[]{:T(128)}, f32[51200]{0:T(1024)S(1)}) fusion(f32[1,51200]{1,0:T(1,128)} %param.7, f32[1,51200]{1,0:T(1,128)} %bitcast.57), kind=kLoop, calls=%fused_computation.22 | loop fusion | flops 153599 | bytes 614404 | tf_op jit(solution)/shard_map/reduce_sum | solution.py:95
  3.1 0.1 reshape.104
  3.2 2.6 %convolution_bitcast_fusion.1 = f32[320,160]{0,1:T(8,128)S(1)} fusion(f32[320,160]{1,0:T(8,128)S(1)} %reshape.104, f32[320]{0:T(512)S(1)} %add_multiply_fusion, pred[320]{0:T(512)(128)(4,1)S(1)} %iota_compare_fusion), kind=kOutput, calls=%fused_computation.5 | convolution fusion | flops 197120000 | bytes 411200 | tf_op jit(solution)/shard_map/kn,mkl->mnl/dot_general | solution.py:58
  5.8 1.1 convolution_convert_fusion
  6.9 0.1 copy.14
  7.0 0.3 convert_element_type.33
  7.3 0.0 copy-start.2
  7.3 0.5 broadcast.94
  7.9 0.0 copy-start.6
  7.9 0.0 copy-start.7
  7.9 1.3 reduce.14
  9.2 0.2 reshape.146
  9.3 23.1 %all_to_all.36 = bf16[32,2,800]{2,1,0:T(2,128)(2,1)S(1)} all-to-all(bf16[32,2,800]{2,1,0:T(2,128)(2,1)S(1)} %reshape.146), channel_id=1, replica_groups=mesh['tm_0'=2,'tm_1'=4,'space_0'=4,'space_1'=4,'space_2'=2] {'space_0','..., dimensions={0} | all-to-all | bytes 204800 | tf_op jit(solution)/shard_map/all_to_all | solution.py:82
  32.5 0.2 reshape.147
  32.7 1.0 broadcast_in_dim.57
  33.6 4.5 %all-to-all-start.1 = ((bf16[8,32,1600]{2,1,0:T(8,128)(2,1)}), bf16[8,32,1600]{2,1,0:T(8,128)(2,1)S(1)}, u32[]{:S(2)}, u32[]{:S(2)}) async-start(bf16[8,32,1600]{2,1,0:T(8,128)(2,1)} %broadcast_in_dim.57), calls=%async_computation.1 | async-start | bytes 1703936 | tf_op jit(solution)/shard_map/all_to_all | solution.py:22
  38.2 0.0 copy-done.2
  38.2 0.0 copy-done.6
  38.2 0.1 multiply_reduce_fusion.5
  38.3 0.0 copy-done.7
  38.4 0.1 and_reduce_fusion
  38.5 12.5 %all-to-all-done.1 = bf16[8,32,1600]{2,1,0:T(8,128)(2,1)S(1)} async-done(((bf16[8,32,1600]{2,1,0:T(8,128)(2,1)}), bf16[8,32,1600]{2,1,0:T(8,128)(2,1)S(1)}, u32[]{:S(2)}, u32[]{:S(2)}) %all-to-all-start.1) | async-done | bytes 819232 | tf_op jit(solution)/shard_map/all_to_all | solution.py:22
  50.9 0.2 bitcast_convert_fusion
  51.1 0.7 copy.34
  51.9 4.7 %multiply_reduce_fusion.1 = f32[1600,2,4]{0,2,1:T(4,128)S(1)} fusion(f32[1600,256]{1,0:T(8,128)S(1)} %copy.34, bf16[2,256,4,1600]{1,3,2,0:T(8,128)(2,1)} %param.9), kind=kLoop, calls=%fused_computation.3 | loop fusion | flops 9817600 | bytes 8243200 | tf_op jit(solution)/shard_map/dzab,zb->dab/dot_general | solution.py:84
  56.6 0.1 reshape.107
  56.7 0.0 copy-start.3
  56.7 0.0 copy-start.4
  56.7 0.0 copy-start.5
  56.7 34.9 %gather_fusion = f32[4096]{0:T(1024)S(1)} fusion(f32[2,6400]{1,0:T(2,128)S(1)} %reshape.107, s32[4096]{0:T(1024)S(1)} %bitcast.53), kind=kCustom, calls=%fused_computation | custom fusion | bytes 65536 | tf_op jit(solution)/shard_map/jit(take_along_axis)/gather | solution.py:91
  91.7 0.0 copy-done.3
  91.7 0.0 copy-done.4
  91.7 0.0 copy-done.5
  91.7 0.8 fusion.26
  92.5 22.1 %scatter_custom_fusion = f32[12800]{0:T(1024)S(1)} fusion(s32[4096]{0:T(1024)S(1)} %bitcast.62, f32[4096]{0:T(1024)S(1)} %bitcast.63, f32[]{:T(128)} %constant.18.clone.1), kind=kCustom, calls=%fused_computation.44 | custom fusion | flops 4096 | bytes 51204
  114.6 0.1 reshape.109
  114.7 4.8 %multiply_reduce_fusion = bf16[1600,256]{1,0:T(8,128)(2,1)S(1)} fusion(f32[1600,2,4]{0,2,1:T(4,128)S(1)} %bitcast_convert_fusion.1, bf16[2,256,4,1600]{1,3,2,0:T(8,128)(2,1)} %param.9), kind=kLoop, calls=%fused_computation.2 | loop fusion | flops 9420800 | bytes 7424000
  119.5 0.7 copy.31
  120.2 16.1 %all_to_all.37 = bf16[8,32,1600]{2,1,0:T(8,128)(2,1)S(1)} all-to-all(bf16[8,32,1600]{2,1,0:T(8,128)(2,1)S(1)} %bitcast.54), channel_id=1, replica_groups=mesh['tm_0'=2,'tm_1'=4,'space_0'=4,'space_1'=4,'space_2'=2] {'tm_0','tm_1'}, dimensions={0} | all-to-all | bytes 1638400 | tf_op jit(solution)/shard_map/all_to_all | solution.py:37
  136.4 0.1 reduce_sum.41
  136.5 0.0 copy-start.1
  136.5 0.7 reduce.15
  137.2 0.0 copy-start
  137.2 0.8 reshape.148
  138.0 5.6 %all-to-all-start.3 = ((bf16[32,2,800]{2,1,0:T(2,128)(2,1)}), bf16[32,2,800]{2,1,0:T(2,128)(2,1)S(1)}, u32[]{:S(2)}, u32[]{:S(2)}) async-start(bf16[32,2,800]{2,1,0:T(2,128)(2,1)} %reshape.148), calls=%async_computation.3 | async-start | bytes 229376 | tf_op jit(solution)/shard_map/all_to_all | solution.py:107
  145.0 9.2 %all-to-all-done.3 = bf16[32,2,800]{2,1,0:T(2,128)(2,1)S(1)} async-done(((bf16[32,2,800]{2,1,0:T(2,128)(2,1)}), bf16[32,2,800]{2,1,0:T(2,128)(2,1)S(1)}, u32[]{:S(2)}, u32[]{:S(2)}) %all-to-all-start.3) | async-done | bytes 102432 | tf_op jit(solution)/shard_map/all_to_all | solution.py:107
  154.3 0.2 reshape.149
  154.4 0.7 reduce.6
  155.1 0.2 reshape.111
  155.3 2.3 %convolution_bitcast_fusion = f32[320,160]{0,1:T(8,128)S(1)} fusion(bf16[320,160]{1,0:T(8,128)(2,1)S(1)} %reshape.111, f32[320]{0:T(512)S(1)} %add_multiply_fusion, pred[320]{0:T(512)(128)(4,1)S(1)} %iota_compare_fusion), kind=kOutput, calls=%fused_computation.4 | convolution fusion | flops 197120000 | bytes 308800 | tf_op jit(solution)/shard_map/kn,mnp->mkp/dot_general | solution.py:65
  157.6 1.3 fusion.10
  158.9 0.3 reshape.113
  159.2 0.0 copy-done.1
  159.2 0.0 copy-done
  159.2 1.0 multiply_reduce_fusion.2
  160.3 4.4 %all-reduce.4 = (f32[]{:T(128)}, f32[]{:T(128)}) all-reduce(f32[]{:T(128)S(6)} %add.87, f32[]{:T(128)} %get-tuple-element.14), channel_id=1, replica_groups=mesh['tm_0'=2,'tm_1'=4,'space_0'=4,'space_1'=4,'space_2'=2] {'tm_0'}, use_global_device_ids=true, to_apply=%region_1.2 | all-reduce | flops 2 | bytes 16 | tf_op jit(solution)/shard_map/psum | solution.py:43
  164.7 7.7 %all-reduce.2 = (f32[]{:T(128)}, f32[]{:T(128)}) all-reduce(f32[]{:T(128)} %get-tuple-element.12, f32[]{:T(128)} %get-tuple-element.13), channel_id=1, replica_groups=mesh['tm_0'=2,'tm_1'=4,'space_0'=4,'space_1'=4,'space_2'=2] {'tm_1'}, use_global_device_ids=true, to_apply=%region_2.3 | all-reduce | flops 2 | bytes 16 | tf_op jit(solution)/shard_map/psum | solution.py:43
  172.4 8.3 %all-reduce.1 = (f32[]{:T(128)}, f32[]{:T(128)}) all-reduce(f32[]{:T(128)} %get-tuple-element.8, f32[]{:T(128)} %get-tuple-element.9), channel_id=1, replica_groups=mesh['tm_0'=2,'tm_1'=4,'space_0'=4,'space_1'=4,'space_2'=2] {'space_0'}, use_global_device_ids=true, to_apply=%region_3.4 | all-reduce | flops 2 | bytes 16 | tf_op jit(solution)/shard_map/psum | solution.py:43
  180.7 7.0 %all-reduce = (f32[]{:T(128)}, f32[]{:T(128)}) all-reduce(f32[]{:T(128)} %get-tuple-element.6, f32[]{:T(128)} %get-tuple-element.7), channel_id=1, replica_groups=mesh['tm_0'=2,'tm_1'=4,'space_0'=4,'space_1'=4,'space_2'=2] {'space_1'}, use_global_device_ids=true, to_apply=%region_4.5 | all-reduce | flops 2 | bytes 16 | tf_op jit(solution)/shard_map/psum | solution.py:43
  187.7 10.6 %all-reduce.3 = (f32[]{:T(128)}, f32[]{:T(128)}) all-reduce(f32[]{:T(128)} %get-tuple-element.4, f32[]{:T(128)} %get-tuple-element.5), channel_id=1, replica_groups=mesh['tm_0'=2,'tm_1'=4,'space_0'=4,'space_1'=4,'space_2'=2] {'space_2'}, use_global_device_ids=true, to_apply=%region_5.6 | all-reduce | flops 2 | bytes 16 | tf_op jit(solution)/shard_map/psum | solution.py:43
  199.5 0.9 multiply_subtract_fusion
  (17 shorter events, 0.2 us)
Async XLA Ops:
  7.3 30.8 %copy-start.2 = (s32[2,2048]{1,0:T(2,128)S(1)}, s32[2,2048]{1,0:T(2,128)}, u32[]{:S(2)}) copy-start(s32[2,2048]{1,0:T(2,128)} %param.10) | copy-start | bytes 49156
  7.9 30.4 %copy-start.6 = (s32[2]{0:T(128)S(1)}, s32[2]{0:T(128)}, u32[]{:S(2)}) copy-start(s32[2]{0:T(128)} %constant.65) | copy-start | bytes 28
  7.9 30.5 %copy-start.7 = (s32[2]{0:T(128)S(1)}, s32[2]{0:T(128)}, u32[]{:S(2)}) copy-start(s32[2]{0:T(128)} %constant.68) | copy-start | bytes 28
  33.6 17.3 %all-to-all-start.1 = ((bf16[8,32,1600]{2,1,0:T(8,128)(2,1)}), bf16[8,32,1600]{2,1,0:T(8,128)(2,1)S(1)}, u32[]{:S(2)}, u32[]{:S(2)}) async-start(bf16[8,32,1600]{2,1,0:T(8,128)(2,1)} %broadcast_in_dim.57), calls=%async_computation.1 | async-start | bytes 1703936 | tf_op jit(solution)/shard_map/all_to_all | solution.py:22
  56.7 35.0 %copy-start.3 = (f32[2,2048]{1,0:T(2,128)S(1)}, f32[2,2048]{1,0:T(2,128)}, u32[]{:S(2)}) copy-start(f32[2,2048]{1,0:T(2,128)} %param.12) | copy-start | bytes 49156
  56.7 35.0 %copy-start.4 = (f32[2,2048]{1,0:T(2,128)S(1)}, f32[2,2048]{1,0:T(2,128)}, u32[]{:S(2)}) copy-start(f32[2,2048]{1,0:T(2,128)} %param.11) | copy-start | bytes 49156
  56.7 35.0 %copy-start.5 = (s32[2,2048]{1,0:T(2,128)S(1)}, s32[2,2048]{1,0:T(2,128)}, u32[]{:S(2)}) copy-start(s32[2,2048]{1,0:T(2,128)} %param.13) | copy-start | bytes 49156
  136.5 22.7 %copy-start.1 = (f32[51200]{0:T(1024)S(1)}, f32[51200]{0:T(1024)}, u32[]{:S(2)}) copy-start(f32[51200]{0:T(1024)} %param.8) | copy-start | bytes 614404
  137.2 22.0 %copy-start = (f32[1,51200]{1,0:T(1,128)S(1)}, f32[1,51200]{1,0:T(1,128)}, u32[]{:S(2)}) copy-start(f32[1,51200]{1,0:T(1,128)} %param.7) | copy-start | bytes 614404
  138.0 16.2 %all-to-all-start.3 = ((bf16[32,2,800]{2,1,0:T(2,128)(2,1)}), bf16[32,2,800]{2,1,0:T(2,128)(2,1)S(1)}, u32[]{:S(2)}, u32[]{:S(2)}) async-start(bf16[32,2,800]{2,1,0:T(2,128)(2,1)} %reshape.148), calls=%async_computation.3 | async-start | bytes 229376 | tf_op jit(solution)/shard_map/all_to_all | solution.py:107
where the time goes:
time: 201 us; the launch traced here: 200 us
  blocking collectives  77.2 us (38%)
  local copies, waits for them, and re-layouts  40.4 us (20%)
  other arithmetic  40 us (20%)
  waiting for transfers between devices  21.7 us (11%)
  starting transfers between devices  10.2 us (5%)
  matrix products  7.25 us (4%)
  between operations  3.58 us (2%)
    psum x5, blocking collectives, by_axis(): value = lax.psum(value, axis)  38 us
    gather x3, local copies, waits for them, and re-layouts, per_device(): modelled = jnp.take_along_axis(cells_flat, obs_index, axis=1)  34.9 us
    unnamed x10, other arithmetic  28.7 us
    all_to_all x1, blocking collectives, per_device(): lax.all_to_all(member_field, SPACE, split_axis=1, concat_axis=0, tiled=True)  23.1 us
    all_to_all x1, blocking collectives, sent_and_summed(): lax.all_to_all(tiles, axis, split_axis=0, concat_axis=0, tiled=True)  16.1 us
    all_to_all x1, waiting for transfers between devices, from_everyone(): return lax.all_to_all(copies, axis, split_axis=0, concat_axis=0, tiled=True)  12.5 us
    all_to_all x1, waiting for transfers between devices, per_device(): lax.all_to_all(summed_rows.astype(jnp.bfloat16), SPACE, split_axis=0, con...  9.22 us
    all_to_all x1, starting transfers between devices, per_device(): lax.all_to_all(summed_rows.astype(jnp.bfloat16), SPACE, split_axis=0, con...  5.64 us
  transfers between devices with their start and end apart: 2, of which 2 were waited for; matrix products, arithmetic and copies ran while one was open for 0% of the time, Pallas kernels for 0%

commit v1 on v0

--- a/solution.py
+++ b/solution.py
@@ -1,6 +1,8 @@
 import jax
 import jax.numpy as jnp
 from jax import lax
+from jax.experimental import pallas as pl
+from jax.experimental.pallas import tpu as pltpu
 from jax.sharding import Mesh
 from jax.sharding import PartitionSpec as P
 
@@ -11,6 +13,142 @@
 TM_SPACE = ("tm_0", "tm_1", "space_0", "space_1", "space_2")
 
 
+PIECE = 1600
+LEV = 4
+BLOCKS = 13
+ROWS = 64
+OBS = 2048
+CHUNK = 256
+
+
+def split3(value):
+    first = value.astype(jnp.bfloat16)
+    rest = value - first.astype(jnp.float32)
+    second = rest.astype(jnp.bfloat16)
+    third = (rest - second.astype(jnp.float32)).astype(jnp.bfloat16)
+    return first, second, third
+
+
+def middle_kernel(p_ref, f_ref, idx_ref, inn_ref, sig_ref, qc_ref, adj_ref, cost_ref,
+                  cells, table, modelled, grads, where_row, where_lane):
+    f32 = jnp.float32
+    cells[...] = jnp.zeros_like(cells)
+
+    def forward(blk, start, width):
+        rows = p_ref[:, pl.ds(start, width), :].reshape(8 * width, 256)
+        prod = jnp.dot(rows, f_ref[:, pl.ds(start, width)], preferred_element_type=f32)
+        same = lax.broadcasted_iota(jnp.int32, (width, width), 0) == lax.broadcasted_iota(
+            jnp.int32, (width, width), 1)
+        for k in range(8):
+            one = jnp.where(same, prod[k * width:(k + 1) * width], 0.0)
+            row = jnp.sum(one, axis=0, keepdims=True)
+            cells[k // LEV, pl.ds(k % LEV * BLOCKS + blk, 1), 0:width] = row
+
+    def forward_step(blk, carry):
+        forward(blk, pl.multiple_of(blk * 128, 128), 128)
+        return carry
+
+    lax.fori_loop(0, 12, forward_step, 0)
+    forward(12, 1536, 64)
+
+    index = idx_ref[...]
+    level = ((index >= PIECE).astype(jnp.int32) + (index >= 2 * PIECE).astype(jnp.int32)
+             + (index >= 3 * PIECE).astype(jnp.int32))
+    point = index - level * PIECE
+    where_row[...] = level * BLOCKS + (point >> 7)
+    where_lane[...] = point & 127
+
+    for t in range(2):
+        parts = split3(jnp.transpose(cells[t]))
+        for k in range(3):
+            table[t, :, k * ROWS:(k + 1) * ROWS] = parts[k]
+
+    row_id = lax.broadcasted_iota(jnp.int32, (ROWS, CHUNK), 0)
+    lane_id = lax.broadcasted_iota(jnp.int32, (128, CHUNK), 0)
+
+    for t in range(2):
+        def gather_step(c, carry):
+            at = pl.ds(pl.multiple_of(c * CHUNK, CHUNK), CHUNK)
+            hot = jnp.where(row_id == where_row[t:t + 1, at], 1.0, 0.0).astype(jnp.bfloat16)
+            hot = jnp.concatenate([hot, hot, hot], axis=0)
+            lines = jnp.dot(table[t], hot, preferred_element_type=f32)
+            lines = jnp.where(lane_id == where_lane[t:t + 1, at], lines, 0.0)
+            modelled[t:t + 1, at] = jnp.sum(lines, axis=0, keepdims=True)
+            return carry
+        lax.fori_loop(0, OBS // CHUNK, gather_step, 0)
+
+    sigma = sig_ref[...]
+    kind = qc_ref[...]
+    radius_sq = jnp.where(kind == 0, 16.0, jnp.where(kind == 1, 4.0, 1.0))
+    scaled = (modelled[...] - inn_ref[...]) / sigma
+    scaled_sq = scaled * scaled / radius_sq
+    terms = 0.5 * radius_sq * jnp.log1p(scaled_sq)
+    cost_ref[...] = jnp.sum(terms, axis=(0, 1), keepdims=True)
+    grad = scaled / ((1.0 + scaled_sq) * sigma)
+    first, second, third = split3(grad)
+    grads[0] = first.astype(f32)
+    grads[1] = second.astype(f32)
+    grads[2] = third.astype(f32)
+
+    sums = []
+    for t in range(2):
+        def scatter_step(c, total):
+            at = pl.ds(pl.multiple_of(c * CHUNK, CHUNK), CHUNK)
+            hot = row_id == where_row[t:t + 1, at]
+            left = jnp.concatenate(
+                [jnp.where(hot, grads[k, t:t + 1, at], 0.0).astype(jnp.bfloat16) for k in range(3)],
+                axis=0)
+            right = jnp.where(lane_id == where_lane[t:t + 1, at], 1.0, 0.0).astype(jnp.bfloat16)
+            return total + lax.dot_general(left, right, (((1,), (1,)), ((), ())),
+                                           preferred_element_type=f32)
+        total = lax.fori_loop(0, OBS // CHUNK, scatter_step, jnp.zeros((3 * ROWS, 128), f32))
+        sums.append(total[0:ROWS] + total[ROWS:2 * ROWS] + total[2 * ROWS:3 * ROWS])
+    update = jnp.concatenate(sums, axis=0).astype(jnp.bfloat16).astype(f32)
+    columns = jnp.transpose(update)
+
+    def backward(cols, start, width):
+        for half in range(width // 64):
+            total = jnp.zeros((64, 256), f32)
+            for k in range(8):
+                j = k // LEV * ROWS + k % LEV * BLOCKS
+                weight = cols[half * 64:(half + 1) * 64, j:j + 1]
+                total = total + p_ref[k, pl.ds(start + half * 64, 64), :].astype(f32) * weight
+            yield total
+
+    def backward_step(blk, carry):
+        start = pl.multiple_of(blk * 128, 128)
+        cols = pltpu.roll(columns, 128 - blk, axis=1)
+        total = jnp.concatenate(list(backward(cols, start, 128)), axis=0)
+        adj_ref[:, pl.ds(start, 128)] = jnp.transpose(total).astype(jnp.bfloat16)
+        return carry
+
+    lax.fori_loop(0, 12, backward_step, 0)
+    cols = pltpu.roll(columns, 128 - 12, axis=1)
+    (total,) = backward(cols, 1536, 64)
+    adj_ref[:, 1536:1600] = jnp.transpose(total).astype(jnp.bfloat16)
+
+
+def middle(cases, fields, obs_index, innovation, obs_sigma, qc_class):
+    vm = pl.BlockSpec(memory_space=pltpu.VMEM)
+    return pl.pallas_call(
+        middle_kernel,
+        out_shape=(jax.ShapeDtypeStruct((256, PIECE), jnp.bfloat16),
+                   jax.ShapeDtypeStruct((1, 1), jnp.float32)),
+        in_specs=[vm] * 6,
+        out_specs=(vm, vm),
+        scratch_shapes=[
+            pltpu.VMEM((2, ROWS, 128), jnp.float32),
+            pltpu.VMEM((2, 128, 3 * ROWS), jnp.bfloat16),
+            pltpu.VMEM((2, OBS), jnp.float32),
+            pltpu.VMEM((3, 2, OBS), jnp.float32),
+            pltpu.VMEM((2, OBS), jnp.int32),
+            pltpu.VMEM((2, OBS), jnp.int32),
+        ],
+        compiler_params=pltpu.CompilerParams(vmem_limit_bytes=40 * 1024 * 1024),
+        name="middle",
+    )(cases, fields, obs_index, innovation, obs_sigma, qc_class)
+
+
 def joined_along(tiles, dim):
     lengths = list(tiles.shape[1:])
     lengths[dim] *= tiles.shape[0]
@@ -36,12 +174,6 @@
     tiles = cut_along(value, dim, lax.axis_size(axis))
     arrived = lax.all_to_all(tiles, axis, split_axis=0, concat_axis=0, tiled=True)
     return arrived.astype(jnp.float32).sum(axis=0)
-
-
-def by_axis(value, axes):
-    for axis in axes:
-        value = lax.psum(value, axis)
-    return value
 
 
 def lookup_tables(segment_length):
@@ -70,53 +202,24 @@
 def per_device(control, spectrum, perturb, obs_index, innovation, obs_sigma, qc_class):
     basis_x = lookup_tables(GX)
     basis_y = lookup_tables(GY)
-    slot_count = perturb.shape[0]
-    levels = perturb.shape[2]
-    piece_len = perturb.shape[3]
-    radius = jnp.where(qc_class == 0, 4.0, jnp.where(qc_class == 1, 2.0, 1.0)).astype(jnp.float32)
-
-    def scatter_cells(indices, values):
-        return jnp.zeros((levels * piece_len,), jnp.float32).at[indices].add(values)
-
+    cases = perturb.transpose(0, 2, 3, 1).reshape(2 * LEV, PIECE, 256)
     member_field = synthesize(control, spectrum, basis_x, basis_y).astype(jnp.bfloat16)
     pieces = lax.all_to_all(member_field, SPACE, split_axis=1, concat_axis=0, tiled=True)
-    selected_entries = perturb
-    increment = jnp.einsum(
-        "dzab,zb->dab",
-        selected_entries,
-        gather_directly(pieces, TM, 0),
-        preferred_element_type=jnp.float32,
-    )
-    cells_flat = increment.reshape(slot_count, levels * piece_len)
-    modelled = jnp.take_along_axis(cells_flat, obs_index, axis=1)
-    scaled = (modelled - innovation) / obs_sigma
-    scaled_sq = scaled * scaled / (radius * radius)
-    obs_part = jnp.sum(0.5 * radius * radius * jnp.log1p(scaled_sq))
+    fields = gather_directly(pieces, TM, 0)
+    partial, obs_part = middle(cases, fields, obs_index, innovation, obs_sigma, qc_class)
     back_part = 0.5 * jnp.sum(control * control)
-    obs_grad = scaled / ((1.0 + scaled_sq) * obs_sigma)
-    control_update = jax.vmap(scatter_cells)(obs_index, obs_grad).astype(jnp.bfloat16)
-    control_update = control_update.reshape(slot_count, levels, piece_len)
-    selected_entries = perturb
-    summed_rows = sent_and_summed(
-        jnp.einsum(
-            "qiyr,qyr->ir", selected_entries, control_update, preferred_element_type=jnp.float32
-        ).astype(jnp.bfloat16),
-        TM,
-        0,
-    )
+    summed_rows = sent_and_summed(partial, TM, 0)
     adjoint = lax.all_to_all(
         summed_rows.astype(jnp.bfloat16), SPACE, split_axis=0, concat_axis=1, tiled=True
     ).astype(summed_rows.dtype)
     gradient = control + analyze(adjoint, spectrum, basis_x, basis_y)
     grad_part = jnp.sum(gradient * gradient)
-    obs_cost = by_axis(obs_part, TM_SPACE)
-    back_cost = by_axis(back_part, TM_SPACE)
-    grad_sq = by_axis(grad_part, TM_SPACE)
-    total_cost = back_cost + obs_cost
-    step_size = 0.5 * total_cost / (grad_sq + 1e-06)
-    control = control - step_size * gradient
-    cost_list = [total_cost]
-    return (control, jnp.stack(cost_list))
+    mine = jnp.stack([obs_part[0, 0] + back_part, grad_part]).reshape(1, 1, 2)
+    mine = jnp.broadcast_to(mine, (256, 1, 2))
+    sums = lax.all_to_all(mine, TM_SPACE, split_axis=0, concat_axis=0, tiled=True).sum(axis=(0, 1))
+    total_cost = sums[0]
+    step_size = 0.5 * total_cost / (sums[1] + 1e-06)
+    return (control - step_size * gradient, total_cost.reshape(1))
 
 
 def solution(mesh):

time: 201 us -> 130 us (0.65)
  local copies, waits for them, and re-layouts: 40.4 us -> 6.46 us
  other arithmetic: 40 us -> 8.12 us
  Pallas kernels: 0 us -> 15.4 us
  waiting for transfers between devices: 21.7 us -> 9.21 us
  starting transfers between devices: 10.2 us -> 6.1 us
  blocking collectives: 77.2 us -> 73.3 us
    psum x5 -> x0, blocking collectives: 38 us -> none  [by_axis(): value = lax.psum(value, axis)]
    all_to_all x0 -> x2, blocking collectives: none -> 35.3 us  [the longest x1 17.9 us: per_device(): lax.all_to_all(mine, TM_SPACE, split_axis=0, concat_axis=0, tiled=True)]
    gather x3 -> x0, local copies, waits for them, and re-layouts: 34.9 us -> none  [per_device(): modelled = jnp.take_along_axis(cells_flat, obs_index, axis=1)]
    unnamed x10 -> x1, other arithmetic: 28.7 us -> 1.28 us
    pallas_call x0 -> x1, Pallas kernels: none -> 15.4 us  [middle(): pl.pallas_call(middle_kernel, out_shape=(jax.ShapeDtypeStruct((256, PIECE...]
    all_to_all x1 -> x0, waiting for transfers between devices: 12.5 us -> none  [from_everyone(): return lax.all_to_all(copies, axis, split_axis=0, concat_axis=0, tiled=True)]
    dot_general x1 -> x0, other arithmetic: 4.71 us -> none  [per_device(): jnp.einsum('dzab,zb->dab', selected_entries, gather_directly(pieces, TM,...]
    all_to_all x1 -> x0, starting transfers between devices: 4.54 us -> none  [from_everyone(): return lax.all_to_all(copies, axis, split_axis=0, concat_axis=0, tiled=True)]
  transfers between devices with their start and end apart: 2 -> 1, of which waited for: 2 -> 1; matrix products, arithmetic and copies ran while one was open for 0% -> 0% of each run, Pallas kernels for 0% -> 0%
where the time goes in v1:
time: 130 us; the launch traced here: 129 us
  blocking collectives  73.3 us (56%)
  Pallas kernels  15.4 us (12%)
  waiting for transfers between devices  9.21 us (7%)
  other arithmetic  8.12 us (6%)
  matrix products  7.26 us (6%)
  local copies, waits for them, and re-layouts  6.46 us (5%)
  starting transfers between devices  6.1 us (5%)
  between operations  3.53 us (3%)
    all_to_all x1, blocking collectives, per_device(): lax.all_to_all(member_field, SPACE, split_axis=1, concat_axis=0, tiled=True)  23.1 us
    all_to_all x1, blocking collectives, per_device(): lax.all_to_all(mine, TM_SPACE, split_axis=0, concat_axis=0, tiled=True)  17.9 us
    all_to_all x1, blocking collectives, from_everyone(): return lax.all_to_all(copies, axis, split_axis=0, concat_axis=0, tiled=True)  17.4 us
    pallas_call x1, Pallas kernels, middle(): pl.pallas_call(middle_kernel, out_shape=(jax.ShapeDtypeStruct((256, PIECE...  15.4 us
    all_to_all x1, blocking collectives, sent_and_summed(): lax.all_to_all(tiles, axis, split_axis=0, concat_axis=0, tiled=True)  14.9 us
    all_to_all x1, waiting for transfers between devices, per_device(): lax.all_to_all(summed_rows.astype(jnp.bfloat16), SPACE, split_axis=0, con...  9.21 us
    all_to_all x1, starting transfers between devices, per_device(): lax.all_to_all(summed_rows.astype(jnp.bfloat16), SPACE, split_axis=0, con...  6.1 us
    unnamed x20, local copies, waits for them, and re-layouts  4.73 us
  transfers between devices with their start and end apart: 1, of which 1 were waited for; matrix products, arithmetic and copies ran while one was open for 0% of the time, Pallas kernels for 0%

profile of v1, /device:TPU:1, one launch (start us, length us, event | category | flops | bytes accessed | tf_op | source)
XLA Modules:
  0.0 129.4 jit_solution(6692384776384616247)
XLA Ops:
  0.6 0.0 copy-start.4
  0.6 0.0 copy-start.3
  0.7 0.0 copy-start.2
  0.7 0.0 copy-start.1
  0.7 2.4 %multiply_reduce_fusion.1 = (f32[]{:T(128)}, f32[51200]{0:T(1024)S(1)}) fusion(f32[1,51200]{1,0:T(1,128)} %param.7, f32[1,51200]{1,0:T(1,128)} %bitcast.38), kind=kLoop, calls=%fused_computation.16 | loop fusion | flops 153599 | bytes 614404 | tf_op jit(solution)/shard_map/reduce_sum | solution.py:210
  3.1 0.1 reshape.102
  3.3 2.6 %convolution_bitcast_fusion.1 = f32[320,160]{0,1:T(8,128)S(1)} fusion(f32[320,160]{1,0:T(8,128)S(1)} %reshape.102, f32[320]{0:T(512)S(1)} %add_multiply_fusion, pred[320]{0:T(512)(128)(4,1)S(1)} %iota_compare_fusion), kind=kOutput, calls=%fused_computation.1 | convolution fusion | flops 197120000 | bytes 411200 | tf_op jit(solution)/shard_map/kn,mkl->mnl/dot_general | solution.py:190
  5.9 1.1 convolution_convert_fusion
  7.0 0.1 copy.22
  7.1 0.3 convert_element_type.20
  7.4 0.5 broadcast.40
  7.9 1.3 reduce.6
  9.2 0.2 reshape.117
  9.4 23.1 %all_to_all.41 = bf16[32,2,800]{2,1,0:T(2,128)(2,1)S(1)} all-to-all(bf16[32,2,800]{2,1,0:T(2,128)(2,1)S(1)} %reshape.117), channel_id=1, replica_groups=mesh['tm_0'=2,'tm_1'=4,'space_0'=4,'space_1'=4,'space_2'=2] {'space_0','..., dimensions={0} | all-to-all | bytes 204800 | tf_op jit(solution)/shard_map/all_to_all | solution.py:207
  32.5 0.2 reshape.118
  32.6 0.1 broadcast_in_dim.39
  32.7 17.4 %all_to_all.42 = bf16[8,32,1600]{2,1,0:T(8,128)(2,1)S(1)} all-to-all(bf16[8,32,1600]{2,1,0:T(8,128)(2,1)S(1)} %broadcast_in_dim.39), channel_id=1, replica_groups=mesh['tm_0'=2,'tm_1'=4,'space_0'=4,'space_1'=4,'space_2'=2] {'tm_0','tm_1'}, dimensions={0} | all-to-all | bytes 1638400 | tf_op jit(solution)/shard_map/all_to_all | solution.py:160
  50.1 0.0 copy-done.4
  50.1 0.0 copy-done.3
  50.1 0.0 copy-done.2
  50.1 0.0 copy-done.1
  50.1 0.0 copy-start
  50.1 2.9 %copy-done = bf16[2,256,4,1600]{1,3,2,0:T(8,128)(2,1)S(1)} copy-done((bf16[2,256,4,1600]{1,3,2,0:T(8,128)(2,1)S(1)}, bf16[2,256,4,1600]{1,3,2,0:T(8,128)(2,1)}, u32[]{:S(2)}) %copy-start) | copy-done | bytes 6553624
  53.0 0.0 copy-start.6
  53.0 0.0 copy-start.5
  53.0 15.4 %middle.1 = (bf16[256,1600]{1,0:T(8,128)(2,1)S(1)}, f32[1,1]{1,0:T(1,128)}) custom-call(bf16[8,1600,256]{2,1,0:T(8,128)(2,1)S(1)} %bitcast.33, bf16[256,1600]{1,0:T(8,128)(2,1)S(1)} %bitcast.34, s32[2,2048]{1,0:T(2,128)S(1)} %copy-done.1, f32[2,2048]{1,0:T(2,128)S(1)} %copy-done.2, f32[2,2048]{1,0:T(2,128)S(1)} %copy-done.3, s32[2,2048]{1,0:T(2,128)S(1)} %copy-done.4), custom_call_target="tpu_custom_call" | custom-call | tf_op jit(solution)/shard_map/middle/pallas_call | solution.py:133
  68.4 14.9 %all_to_all.43 = bf16[8,32,1600]{2,1,0:T(8,128)(2,1)S(1)} all-to-all(bf16[8,32,1600]{2,1,0:T(8,128)(2,1)S(1)} %bitcast.35), channel_id=1, replica_groups=mesh['tm_0'=2,'tm_1'=4,'space_0'=4,'space_1'=4,'space_2'=2] {'tm_0','tm_1'}, dimensions={0} | all-to-all | bytes 1638400 | tf_op jit(solution)/shard_map/all_to_all | solution.py:175
  83.3 0.1 reduce_sum.40
  83.5 0.7 reduce.7
  84.1 0.8 reshape.119
  85.0 6.1 %all-to-all-start.3 = ((bf16[32,2,800]{2,1,0:T(2,128)(2,1)}), bf16[32,2,800]{2,1,0:T(2,128)(2,1)S(1)}, u32[]{:S(2)}, u32[]{:S(2)}) async-start(bf16[32,2,800]{2,1,0:T(2,128)(2,1)} %reshape.119), calls=%async_computation.3 | async-start | bytes 229376 | tf_op jit(solution)/shard_map/all_to_all | solution.py:212
  92.4 9.2 %all-to-all-done.3 = bf16[32,2,800]{2,1,0:T(2,128)(2,1)S(1)} async-done(((bf16[32,2,800]{2,1,0:T(2,128)(2,1)}), bf16[32,2,800]{2,1,0:T(2,128)(2,1)S(1)}, u32[]{:S(2)}, u32[]{:S(2)}) %all-to-all-start.3) | async-done | bytes 102432 | tf_op jit(solution)/shard_map/all_to_all | solution.py:212
  101.6 0.2 reshape.120
  101.8 0.6 reduce.2
  102.4 0.2 reshape.106
  102.6 2.3 %convolution_bitcast_fusion = f32[320,160]{0,1:T(8,128)S(1)} fusion(bf16[320,160]{1,0:T(8,128)(2,1)S(1)} %reshape.106, f32[320]{0:T(512)S(1)} %add_multiply_fusion, pred[320]{0:T(512)(128)(4,1)S(1)} %iota_compare_fusion), kind=kOutput, calls=%fused_computation | convolution fusion | flops 197120000 | bytes 308800 | tf_op jit(solution)/shard_map/kn,mnp->mkp/dot_general | solution.py:197
  105.0 1.3 fusion.10
  106.3 0.3 reshape.108
  106.5 0.0 copy-done.6
  106.6 0.0 copy-done.5
  106.6 1.0 multiply_reduce_fusion
  107.6 0.7 pad_maximum_fusion
  108.3 0.1 broadcast_in_dim.40
  108.4 17.9 %all_to_all.44 = f32[256,1,2]{2,1,0:T(1,128)S(1)} all-to-all(f32[256,1,2]{2,1,0:T(1,128)S(1)} %broadcast_in_dim.40), channel_id=1, replica_groups=mesh['tm_0'=2,'tm_1'=4,'space_0'=4,'space_1'=4,'space_2'=2] {'tm_0','tm_..., dimensions={0} | all-to-all | bytes 4096 | tf_op jit(solution)/shard_map/all_to_all | solution.py:219
  126.3 0.3 reduce_sum.42
  126.6 0.6 fusion.33
  128.5 0.9 multiply_subtract_fusion
  (6 shorter events, 0.1 us)
Async XLA Ops:
  0.6 49.5 %copy-start.4 = (s32[2,2048]{1,0:T(2,128)S(1)}, s32[2,2048]{1,0:T(2,128)}, u32[]{:S(2)}) copy-start(s32[2,2048]{1,0:T(2,128)} %qc_ref.1) | copy-start | bytes 49156
  0.6 49.5 %copy-start.3 = (f32[2,2048]{1,0:T(2,128)S(1)}, f32[2,2048]{1,0:T(2,128)}, u32[]{:S(2)}) copy-start(f32[2,2048]{1,0:T(2,128)} %sig_ref.1) | copy-start | bytes 49156
  0.7 49.5 %copy-start.2 = (f32[2,2048]{1,0:T(2,128)S(1)}, f32[2,2048]{1,0:T(2,128)}, u32[]{:S(2)}) copy-start(f32[2,2048]{1,0:T(2,128)} %inn_ref.1) | copy-start | bytes 49156
  0.7 49.5 %copy-start.1 = (s32[2,2048]{1,0:T(2,128)S(1)}, s32[2,2048]{1,0:T(2,128)}, u32[]{:S(2)}) copy-start(s32[2,2048]{1,0:T(2,128)} %idx_ref.1) | copy-start | bytes 49156
  50.1 2.9 %copy-start = (bf16[2,256,4,1600]{1,3,2,0:T(8,128)(2,1)S(1)}, bf16[2,256,4,1600]{1,3,2,0:T(8,128)(2,1)}, u32[]{:S(2)}) copy-start(bf16[2,256,4,1600]{1,3,2,0:T(8,128)(2,1)} %param.9) | copy-start | bytes 19660804
  53.0 53.5 %copy-start.6 = (f32[51200]{0:T(1024)S(1)}, f32[51200]{0:T(1024)}, u32[]{:S(2)}) copy-start(f32[51200]{0:T(1024)} %param.8) | copy-start | bytes 614404
  53.0 53.6 %copy-start.5 = (f32[1,51200]{1,0:T(1,128)S(1)}, f32[1,51200]{1,0:T(1,128)}, u32[]{:S(2)}) copy-start(f32[1,51200]{1,0:T(1,128)} %param.7) | copy-start | bytes 614404
  85.0 16.7 %all-to-all-start.3 = ((bf16[32,2,800]{2,1,0:T(2,128)(2,1)}), bf16[32,2,800]{2,1,0:T(2,128)(2,1)S(1)}, u32[]{:S(2)}, u32[]{:S(2)}) async-start(bf16[32,2,800]{2,1,0:T(2,128)(2,1)} %reshape.119), calls=%async_computation.3 | async-start | bytes 229376 | tf_op jit(solution)/shard_map/all_to_all | solution.py:212

commit v2 on v1

v2 whole, which is shorter than its diff:
```python
import jax
import jax.numpy as jnp
import ml_dtypes
import numpy as np
from jax import lax
from jax.experimental import pallas as pl
from jax.experimental.pallas import tpu as pltpu
from jax.sharding import Mesh
from jax.sharding import PartitionSpec as P

PIECE = 1600
LEV = 4
BLOCKS = 13
ROWS = 64
OBS = 2048
CHUNK = 256


def split3(value):
    first = value.astype(jnp.bfloat16)
    rest = value - first.astype(jnp.float32)
    second = rest.astype(jnp.bfloat16)
    third = (rest - second.astype(jnp.float32)).astype(jnp.bfloat16)
    return first, second, third


def middle_kernel(p_ref, f_ref, idx_ref, inn_ref, sig_ref, qc_ref, adj_ref, cost_ref,
                  cells, table, modelled, grads, where_row, where_lane):
    f32 = jnp.float32
    cells[...] = jnp.zeros_like(cells)

    def forward(blk, start, width):
        rows = p_ref[:, start:start + width, :].reshape(8 * width, 256)
        prod = jnp.dot(rows, f_ref[:, start:start + width], preferred_element_type=f32)
        same = lax.broadcasted_iota(jnp.int32, (width, width), 0) == lax.broadcasted_iota(
            jnp.int32, (width, width), 1)
        for k in range(8):
            one = jnp.where(same, prod[k * width:(k + 1) * width], 0.0)
            row = jnp.sum(one, axis=0, keepdims=True)
            at = k % LEV * BLOCKS + blk
            cells[k // LEV, at:at + 1, 0:width] = row

    for blk in range(BLOCKS):
        forward(blk, blk * 128, min(128, PIECE - blk * 128))

    index = idx_ref[...]
    level = ((index >= PIECE).astype(jnp.int32) + (index >= 2 * PIECE).astype(jnp.int32)
             + (index >= 3 * PIECE).astype(jnp.int32))
    point = index - level * PIECE
    where_row[...] = level * BLOCKS + (point >> 7)
    where_lane[...] = point & 127

    for t in range(2):
        parts = split3(jnp.transpose(cells[t]))
        for k in range(3):
            table[t, :, k * ROWS:(k + 1) * ROWS] = parts[k]

    row_id = lax.broadcasted_iota(jnp.int32, (ROWS, CHUNK), 0)
    lane_id = lax.broadcasted_iota(jnp.int32, (128, CHUNK), 0)

    for t in range(2):
        for c in range(OBS // CHUNK):
            at = slice(c * CHUNK, (c + 1) * CHUNK)
            hot = jnp.where(row_id == where_row[t:t + 1, at], 1.0, 0.0).astype(jnp.bfloat16)
            hot = jnp.concatenate([hot, hot, hot], axis=0)
            lines = jnp.dot(table[t], hot, preferred_element_type=f32)
            lines = jnp.where(lane_id == where_lane[t:t + 1, at], lines, 0.0)
            modelled[t:t + 1, at] = jnp.sum(lines, axis=0, keepdims=True)

    sigma = sig_ref[...]
    kind = qc_ref[...]
    radius_sq = jnp.where(kind == 0, 16.0, jnp.where(kind == 1, 4.0, 1.0))
    scaled = (modelled[...] - inn_ref[...]) / sigma
    scaled_sq = scaled * scaled / radius_sq
    terms = 0.5 * radius_sq * jnp.log1p(scaled_sq)
    cost_ref[...] = jnp.sum(terms, axis=(0, 1), keepdims=True)
    grad = scaled / ((1.0 + scaled_sq) * sigma)
    first, second, third = split3(grad)
    grads[0] = first.astype(f32)
    grads[1] = second.astype(f32)
    grads[2] = third.astype(f32)

    sums = []
    for t in range(2):
        total = jnp.zeros((3 * ROWS, 128), f32)
        for c in range(OBS // CHUNK):
            at = slice(c * CHUNK, (c + 1) * CHUNK)
            hot = row_id == where_row[t:t + 1, at]
            left = jnp.concatenate(
                [jnp.where(hot, grads[k, t:t + 1, at], 0.0).astype(jnp.bfloat16) for k in range(3)],
                axis=0)
            right = jnp.where(lane_id == where_lane[t:t + 1, at], 1.0, 0.0).astype(jnp.bfloat16)
            total = total + lax.dot_general(left, right, (((1,), (1,)), ((), ())),
                                            preferred_element_type=f32)
        sums.append(total[0:ROWS] + total[ROWS:2 * ROWS] + total[2 * ROWS:3 * ROWS])
    update = jnp.concatenate(sums, axis=0).astype(jnp.bfloat16).astype(f32)
    columns = jnp.transpose(update)

    for blk in range(BLOCKS):
        start = blk * 128
        width = min(128, PIECE - start)
        halves = []
        for half in range(width // 64):
            lanes = slice(half * 64, half * 64 + 64)
            points = slice(start + half * 64, start + half * 64 + 64)
            total = jnp.zeros((64, 256), f32)
            for k in range(8):
                j = k // LEV * ROWS + k % LEV * BLOCKS + blk
                total = total + p_ref[k, points, :].astype(f32) * columns[lanes, j:j + 1]
            halves.append(total)
        total = jnp.concatenate(halves, axis=0)
        adj_ref[:, start:start + width] = jnp.transpose(total).astype(jnp.bfloat16)


def middle(cases, fields, obs_index, innovation, obs_sigma, qc_class):
    vm = pl.BlockSpec(memory_space=pltpu.VMEM)
    return pl.pallas_call(
        middle_kernel,
        out_shape=(jax.ShapeDtypeStruct((256, PIECE), jnp.bfloat16),
                   jax.ShapeDtypeStruct((1, 1), jnp.float32)),
        in_specs=[vm] * 6,
        out_specs=(vm, vm),
        scratch_shapes=[
            pltpu.VMEM((2, ROWS, 128), jnp.float32),
            pltpu.VMEM((2, 128, 3 * ROWS), jnp.bfloat16),
            pltpu.VMEM((2, OBS), jnp.float32),
            pltpu.VMEM((3, 2, OBS), jnp.float32),
            pltpu.VMEM((2, OBS), jnp.int32),
            pltpu.VMEM((2, OBS), jnp.int32),
        ],
        compiler_params=pltpu.CompilerParams(vmem_limit_bytes=40 * 1024 * 1024),
        name="middle",
    )(cases, fields, obs_index, innovation, obs_sigma, qc_class)


F32 = jnp.float32
BF16 = jnp.bfloat16
GX = 320
GY = 160
MEMBERS = 256
WIDE = 16 * 128
SPACE = ("space_0", "space_1", "space_2")
TM = ("tm_0", "tm_1")
TM_SPACE = ("tm_0", "tm_1", "space_0", "space_1", "space_2")


def two_parts(value):
    high = np.asarray(value, np.float32).astype(ml_dtypes.bfloat16)
    low = (value - high.astype(np.float64)).astype(np.float32).astype(ml_dtypes.bfloat16)
    return high, low


def lookup_table(length):
    wave = np.arange(length)[:, None]
    angle = np.pi * (np.arange(length)[None, :] + 0.5) * wave / length
    return np.cos(angle) * np.sqrt(np.where(wave == 0, 1.0, 2.0) / length)


def split2(value):
    high = value.astype(BF16)
    return high, (value - high.astype(F32)).astype(BF16)


def product(left, right):
    (left_high, left_low), (right_high, right_low) = left, right
    return (jnp.dot(left_high, right_high, preferred_element_type=F32)
            + (jnp.dot(left_low, right_high, preferred_element_type=F32)
               + jnp.dot(left_high, right_low, preferred_element_type=F32)))


def first_kernel(c_ref, s_ref, x_hbm, y_hbm, cases_hbm, out_ref, back_ref, cases_ref, wide, tall, x_ref, y_ref, sems):
    copies = [
        pltpu.make_async_copy(y_hbm, y_ref, sems.at[0]),
        pltpu.make_async_copy(x_hbm, x_ref, sems.at[1]),
        pltpu.make_async_copy(cases_hbm, cases_ref, sems.at[2]),
    ]
    for copy in copies:
        copy.start()
    control = c_ref[...]
    back_ref[...] = 0.5 * jnp.sum(control * control, axis=(0, 1), keepdims=True)
    coeffs = split2(control * s_ref[...])
    wide[:, PIECE:] = jnp.zeros((32, wide.shape[1] - PIECE), F32)
    copies[0].wait()
    rows = split2(product(coeffs, (y_ref[0], y_ref[1])))
    copies[1].wait()
    field = product((x_ref[0], x_ref[1]), rows)
    for i in range(10):
        wide[:, i * GY:(i + 1) * GY] = field[i * 32:(i + 1) * 32]
    for r in range(BLOCKS):
        tall[:, r, :] = wide[:, r * 128:(r + 1) * 128]
    for r in range(BLOCKS, 16):
        tall[:, r, :] = jnp.zeros((32, 128), F32)
    out_ref[...] = tall[...].astype(BF16)
    copies[2].wait()


def spread_kernel(in_ref, out_ref, tall, wide):
    tall[...] = in_ref[...].astype(F32)
    for r in range(BLOCKS):
        wide[:, r * 128:(r + 1) * 128] = tall[:, r, :]
    value = wide[:, 0:PIECE].astype(BF16)
    for k in range(8):
        out_ref[k] = value


def fold_kernel(in_ref, out_ref, tall, wide):
    total = in_ref[0].astype(F32)
    for k in range(1, 8):
        total = total + in_ref[k].astype(F32)
    wide[:, 0:PIECE] = total
    wide[:, PIECE:] = jnp.zeros((32, wide.shape[1] - PIECE), F32)
    for r in range(BLOCKS):
        tall[:, r, :] = wide[:, r * 128:(r + 1) * 128]
    for r in range(BLOCKS, 16):
        tall[:, r, :] = jnp.zeros((32, 128), F32)
    out_ref[...] = tall[...].astype(BF16)


def last_kernel(in_ref, c_ref, s_ref, xh, xl, yh, yl, back_ref, obs_ref, grad_ref, pay_ref, tall, wide, adj):
    tall[...] = in_ref[...].astype(F32)
    for r in range(BLOCKS):
        wide[:, r * 128:(r + 1) * 128] = tall[:, r, :]
    for i in range(10):
        adj[i * 32:(i + 1) * 32, :] = wide[:, i * GY:(i + 1) * GY].astype(BF16)
    part = adj[...]
    rows = (jnp.dot(xh[...], part, preferred_element_type=F32)
            + jnp.dot(xl[...], part, preferred_element_type=F32))
    grad = c_ref[...] + s_ref[...] * product(split2(rows), (yh[...], yl[...]))
    grad_ref[...] = grad
    cost = back_ref[...] + obs_ref[...]
    norm = jnp.sum(grad * grad, axis=(0, 1), keepdims=True)
    lane = lax.broadcasted_iota(jnp.int32, (MEMBERS, 128), 1)
    pay_ref[...] = jnp.where(lane == 0, cost, jnp.where(lane == 1, norm, 0.0))


def step_kernel(pay_ref, c_ref, g_ref, out_ref, cost_ref):
    sums = jnp.sum(pay_ref[...], axis=0, keepdims=True)
    cost = sums[:, 0:1]
    size = 0.5 * cost / (sums[:, 1:2] + 1e-06)
    out_ref[...] = c_ref[...] - size * g_ref[...]
    cost_ref[...] = cost


def call(kernel, outs, scratch, name, specs=None):
    vm = pl.BlockSpec(memory_space=pltpu.VMEM)

    def run(*args):
        ins = [vm] * len(args)
        for at in specs or ():
            ins[at] = pl.BlockSpec(memory_space=pltpu.HBM)
        return pl.pallas_call(
            kernel,
            out_shape=tuple(jax.ShapeDtypeStruct(*out) for out in outs),
            in_specs=ins,
            out_specs=(vm,) * len(outs),
            scratch_shapes=scratch,
            compiler_params=pltpu.CompilerParams(vmem_limit_bytes=40 * 1024 * 1024),
            name=name,
        )(*args)

    return run


def exchanged(value, axis):
    return lax.all_to_all(value, axis, split_axis=0, concat_axis=0, tiled=True)


def per_device(control, spectrum, perturb, obs_index, innovation, obs_sigma, qc_class):
    order = np.arange(GX).reshape(32, 10).T.reshape(-1)
    table_x = lookup_table(GX)[:, order]
    table_y = lookup_table(GY)
    cases = perturb.transpose(0, 2, 3, 1).reshape(2 * LEV, PIECE, MEMBERS)
    control_grid = control.reshape(GX, GY)
    spectrum_grid = spectrum.reshape(GX, GY)
    tall = pltpu.VMEM((32, 16, 128), F32)
    wide = pltpu.VMEM((32, BLOCKS * 128), F32)

    sent, back, cases = call(
        first_kernel,
        (((32, 16, 128), BF16), ((1, 1), F32), (cases.shape, BF16)),
        [wide, tall, pltpu.VMEM((2, GX, GX), BF16), pltpu.VMEM((2, GY, GY), BF16),
         pltpu.SemaphoreType.DMA((3,))],
        "synthesis", specs=(2, 3, 4),
    )(control_grid, spectrum_grid, np.stack(two_parts(table_x.T)), np.stack(two_parts(table_y)), cases)
    pieces = exchanged(sent, SPACE)
    (copies,) = call(spread_kernel, (((8, 32, PIECE), BF16),), [tall, wide], "spread")(pieces)
    fields = exchanged(copies, TM).reshape(MEMBERS, PIECE)
    partial, obs = middle(cases, fields, obs_index, innovation, obs_sigma, qc_class)
    terms = exchanged(partial.reshape(8, 32, PIECE), TM)
    (summed,) = call(fold_kernel, (((32, 16, 128), BF16),), [tall, wide], "fold")(terms)
    adjoint = exchanged(summed, SPACE)
    gradient, mine = call(
        last_kernel,
        (((GX, GY), F32), ((MEMBERS, 128), F32)),
        [tall, wide, pltpu.VMEM((GX, GY), BF16)],
        "analysis",
    )(adjoint, control_grid, spectrum_grid, *two_parts(table_x), *two_parts(table_y.T), back, obs)
    sums = exchanged(mine.reshape(MEMBERS, 1, 128), TM_SPACE).reshape(MEMBERS, 128)
    result, cost = call(
        step_kernel, (((400, 128), F32), ((1, 1), F32)), [], "step"
    )(sums, control.reshape(400, 128), gradient.reshape(400, 128))
    return result.reshape(1, GX * GY), cost.reshape(1)


def solution(mesh):
    split = Mesh(
        mesh.devices.reshape(2, 4, 4, 4, 2), ("tm_0", "tm_1", "space_0", "space_1", "space_2")
    )
    return jax.shard_map(
        per_device,
        mesh=split,
        in_specs=(
            P(TM_SPACE, None),
            P(),
            P(TM, None, None, SPACE),
            P(TM, SPACE),
            P(TM, SPACE),
            P(TM, SPACE),
            P(TM, SPACE),
        ),
        out_specs=(P(TM_SPACE, None), P()),
        check_vma=False,
    )
```

time: 130 us -> 113 us (0.87)
  matrix products: 7.26 us -> 0 us
  other arithmetic: 8.12 us -> 2.06 us
  waiting for transfers between devices: 9.21 us -> 12.6 us
  between operations: 3.53 us -> 0.76 us
  Pallas kernels: 15.4 us -> 12.8 us
    pallas_call x1, Pallas kernels: 15.4 us -> 5.75 us  [middle(): pl.pallas_call(middle_kernel, out_shape=(jax.ShapeDtypeStruct((256, PIECE...]
    dot_general x4 -> x0, matrix products: 7.26 us -> none  [the longest x1 2.56 us: synthesize(): jnp.einsum('kn,mkl->mnl', basis_x, coeffs, precision=lax.Precision.HIGHEST)]
    pallas_call x0 -> x5, Pallas kernels: none -> 7.04 us  [run(): pl.pallas_call(kernel, out_shape=tuple((jax.ShapeDtypeStruct(*out) for ou...]
    reduce_sum x4 -> x0, other arithmetic: 3.85 us -> none  [the longest x1 2.41 us: per_device(): back_part = 0.5 * jnp.sum(control * control)]
    all_to_all x1, waiting for transfers between devices: 9.21 us -> 12.6 us  [exchanged(): return lax.all_to_all(value, axis, split_axis=0, concat_axis=0, tiled=True)]
    all_to_all x2 -> x0, other arithmetic: 1.31 us -> none  [per_device(): lax.all_to_all(summed_rows.astype(jnp.bfloat16), SPACE, split_axis=0, con...]
    unnamed x20 -> x25, local copies, waits for them, and re-layouts: 4.73 us -> 5.35 us
where the time goes in v2:
time: 113 us; the launch traced here: 112 us
  blocking collectives  72.1 us (64%)
  Pallas kernels  12.8 us (11%)
  waiting for transfers between devices  12.6 us (11%)
  local copies, waits for them, and re-layouts  6.84 us (6%)
  starting transfers between devices  5.2 us (5%)
  other arithmetic  2.06 us (2%)
    all_to_all x4, blocking collectives, exchanged(): return lax.all_to_all(value, axis, split_axis=0, concat_axis=0, tiled=True)  72.1 us
    all_to_all x1, waiting for transfers between devices, exchanged(): return lax.all_to_all(value, axis, split_axis=0, concat_axis=0, tiled=True)  12.6 us
    pallas_call x5, Pallas kernels, run(): pl.pallas_call(kernel, out_shape=tuple((jax.ShapeDtypeStruct(*out) for ou...  7.04 us
    pallas_call x1, Pallas kernels, middle(): pl.pallas_call(middle_kernel, out_shape=(jax.ShapeDtypeStruct((256, PIECE...  5.75 us
    unnamed x25, local copies, waits for them, and re-layouts  5.35 us
    all_to_all x1, starting transfers between devices, exchanged(): return lax.all_to_all(value, axis, split_axis=0, concat_axis=0, tiled=True)  5.2 us
  transfers between devices with their start and end apart: 1, of which 1 were waited for; matrix products, arithmetic and copies ran while one was open for 0% of the time, Pallas kernels for 0%

profile of v2, /device:TPU:1, one launch (start us, length us, event | category | flops | bytes accessed | tf_op | source)
XLA Modules:
  0.0 112.4 jit_solution(2886663649158653358)
XLA Ops:
  0.6 0.0 copy-start.11
  0.6 0.0 copy-start.10
  0.7 0.0 copy-start.9
  0.7 0.0 copy-start.8
  0.7 0.5 broadcast.3
  1.2 2.1 %reduce.3 = f32[51200]{0:T(1024)S(1)} reduce(f32[1,51200]{1,0:T(1,128)} %param.13, f32[]{:T(128)} %broadcast.3), dimensions={0}, to_apply=%param.13.reduce_sub_computation.3 | reduce | bytes 409604 | tf_op args[0]
  3.2 0.1 reshape.37.c_ref
  3.4 1.1 reshape.38.s_ref
  4.5 0.0 copy-start
  4.5 2.9 %copy-done = bf16[2,256,4,1600]{1,3,2,0:T(8,128)(2,1)S(1)} copy-done((bf16[2,256,4,1600]{1,3,2,0:T(8,128)(2,1)S(1)}, bf16[2,256,4,1600]{1,3,2,0:T(8,128)(2,1)}, u32[]{:S(2)}) %copy-start) | copy-done | bytes 6553624
  7.4 0.0 copy-start.2
  7.4 1.0 copy-done.2
  8.4 0.0 copy-start.5
  8.4 0.9 copy-done.5
  9.3 2.7 %synthesis.1 = (bf16[32,16,128]{2,1,0:T(8,128)(2,1)S(1)}, f32[1,1]{1,0:T(1,128)}, bf16[8,1600,256]{2,1,0:T(8,128)(2,1)S(1)}) custom-call(f32[320,160]{1,0:T(8,128)S(1)} %reshape.37.c_ref, f32[320,160]{1,0:T(8,128)S(1)} %reshape.38.s_ref, bf16[2,320,320]{2,1,0:T(8,128)(2,1)S(1)} %copy-done.2, bf16[2,160,160]{2,1,0:T(8,128)(2,1)S(1)} %copy-done.5, ...), custom_call_target="tpu_custom_call" | custom-call | tf_op jit(solution)/shard_map/synthesis/pallas_call | solution.py:251
  12.0 23.4 %all_to_all.25.in_ref = bf16[32,16,128]{2,1,0:T(8,128)(2,1)S(1)} all-to-all(bf16[32,16,128]{2,1,0:T(8,128)(2,1)S(1)} %get-tuple-element.12), channel_id=1, replica_groups=mesh['tm_0'=2,'tm_1'=4,'space_0'=4,'space_1'=4,'space_2'=2] {'space_0','..., dimensions={0} | all-to-all | bytes 262144 | tf_op jit(solution)/shard_map/all_to_all | solution.py:265
  35.4 0.0 copy-start.3
  35.4 0.0 copy-start.4
  35.4 0.0 copy-start.6
  35.4 0.0 copy-start.7
  35.4 0.2 spread.1
  35.6 17.5 %all_to_all.26 = bf16[8,32,1600]{2,1,0:T(8,128)(2,1)S(1)} all-to-all(bf16[8,32,1600]{2,1,0:T(8,128)(2,1)S(1)} %spread.1), channel_id=1, replica_groups=mesh['tm_0'=2,'tm_1'=4,'space_0'=4,'space_1'=4,'space_2'=2] {'tm_0','tm_1'}, dimensions={0} | all-to-all | bytes 1638400 | tf_op jit(solution)/shard_map/all_to_all | solution.py:265
  53.1 0.0 copy-start.1
  53.1 0.0 copy-done.11
  53.1 0.0 copy-done.10
  53.1 0.0 copy-done.9
  53.1 0.0 copy-done.8
  53.1 5.8 %middle.1 = (bf16[256,1600]{1,0:T(8,128)(2,1)S(1)}, f32[1,1]{1,0:T(1,128)}) custom-call(bf16[8,1600,256]{2,1,0:T(8,128)(2,1)S(1)} %get-tuple-element.11.p_ref, bf16[256,1600]{1,0:T(8,128)(2,1)S(1)} %bitcast.13, s32[2,2048]{1,0:T(2,128)S(1)} %copy-done.8, f32[2,2048]{1,0:T(2,128)S(1)} %copy-done.9, f32[2,2048]{1,0:T(2,128)S(1)} %copy-done.10, ...), custom_call_target="tpu_custom_call" | custom-call | tf_op jit(solution)/shard_map/middle/pallas_call | solution.py:117
  58.9 14.9 %all_to_all.27.in_ref = bf16[8,32,1600]{2,1,0:T(8,128)(2,1)S(1)} all-to-all(bf16[8,32,1600]{2,1,0:T(8,128)(2,1)S(1)} %bitcast.14), channel_id=1, replica_groups=mesh['tm_0'=2,'tm_1'=4,'space_0'=4,'space_1'=4,'space_2'=2] {'tm_0','tm_1'}, dimensions={0} | all-to-all | bytes 1638400 | tf_op jit(solution)/shard_map/all_to_all | solution.py:265
  73.8 0.3 fold.1
  74.1 16.3 %all_to_all.28.in_ref = bf16[32,16,128]{2,1,0:T(8,128)(2,1)S(1)} all-to-all(bf16[32,16,128]{2,1,0:T(8,128)(2,1)S(1)} %fold.1), channel_id=1, replica_groups=mesh['tm_0'=2,'tm_1'=4,'space_0'=4,'space_1'=4,'space_2'=2] {'space_0','..., dimensions={0} | all-to-all | bytes 262144 | tf_op jit(solution)/shard_map/all_to_all | solution.py:265
  90.4 0.0 copy-done.3
  90.4 0.0 copy-done.4
  90.4 0.0 copy-done.6
  90.4 0.0 copy-done.7
  90.4 3.0 %analysis.1 = (f32[320,160]{1,0:T(8,128)S(1)}, f32[256,128]{1,0:T(8,128)}) custom-call(bf16[32,16,128]{2,1,0:T(8,128)(2,1)S(1)} %all_to_all.28.in_ref, f32[320,160]{1,0:T(8,128)S(1)} %reshape.37.c_ref, f32[320,160]{1,0:T(8,128)S(1)} %reshape.38.s_ref, bf16[320,320]{1,0:T(8,128)(2,1)S(1)} %copy-done.4, bf16[320,320]{1,0:T(8,128)(2,1)S(1)} %copy-done.3, ...), custom_call_target="tpu_custom_call" | custom-call | tf_op jit(solution)/shard_map/analysis/pallas_call | solution.py:251
  93.4 5.2 %all-to-all-start.4 = ((f32[256,1,128]{2,1,0:T(1,128)}), f32[256,1,128]{2,1,0:T(1,128)S(1)}, u32[]{:S(2)}, u32[]{:S(2)}) async-start(f32[256,1,128]{2,1,0:T(1,128)} %bitcast.5), calls=%async_computation.4 | async-start | bytes 262144 | tf_op jit(solution)/shard_map/all_to_all | solution.py:265
  98.6 0.3 reshape.45.g_ref
  98.9 12.6 %all-to-all-done.4 = f32[256,1,128]{2,1,0:T(1,128)S(1)} async-done(((f32[256,1,128]{2,1,0:T(1,128)}), f32[256,1,128]{2,1,0:T(1,128)S(1)}, u32[]{:S(2)}, u32[]{:S(2)}) %all-to-all-start.4) | async-done | bytes 131104 | tf_op jit(solution)/shard_map/all_to_all | solution.py:265
  111.5 0.0 copy-done.1
  111.5 0.9 step.1
Async XLA Ops:
  0.6 52.5 %copy-start.11 = (s32[2,2048]{1,0:T(2,128)S(1)}, s32[2,2048]{1,0:T(2,128)}, u32[]{:S(2)}) copy-start(s32[2,2048]{1,0:T(2,128)} %qc_ref.1) | copy-start | bytes 49156
  0.6 52.5 %copy-start.10 = (f32[2,2048]{1,0:T(2,128)S(1)}, f32[2,2048]{1,0:T(2,128)}, u32[]{:S(2)}) copy-start(f32[2,2048]{1,0:T(2,128)} %sig_ref.1) | copy-start | bytes 49156
  0.7 52.5 %copy-start.9 = (f32[2,2048]{1,0:T(2,128)S(1)}, f32[2,2048]{1,0:T(2,128)}, u32[]{:S(2)}) copy-start(f32[2,2048]{1,0:T(2,128)} %inn_ref.1) | copy-start | bytes 49156
  0.7 52.5 %copy-start.8 = (s32[2,2048]{1,0:T(2,128)S(1)}, s32[2,2048]{1,0:T(2,128)}, u32[]{:S(2)}) copy-start(s32[2,2048]{1,0:T(2,128)} %idx_ref.1) | copy-start | bytes 49156
  4.5 2.9 %copy-start = (bf16[2,256,4,1600]{1,3,2,0:T(8,128)(2,1)S(1)}, bf16[2,256,4,1600]{1,3,2,0:T(8,128)(2,1)}, u32[]{:S(2)}) copy-start(bf16[2,256,4,1600]{1,3,2,0:T(8,128)(2,1)} %param.15) | copy-start | bytes 19660804
  7.4 1.0 copy-start.2
  8.4 0.9 copy-start.5
  35.4 55.0 %copy-start.3 = (bf16[320,320]{1,0:T(8,128)(2,1)S(1)}, bf16[320,320]{1,0:T(8,128)(2,1)}, u32[]{:S(2)}) copy-start(bf16[320,320]{1,0:T(8,128)(2,1)} %constant.15.clone.xl) | copy-start | bytes 614404
  35.4 55.0 %copy-start.4 = (bf16[320,320]{1,0:T(8,128)(2,1)S(1)}, bf16[320,320]{1,0:T(8,128)(2,1)}, u32[]{:S(2)}) copy-start(bf16[320,320]{1,0:T(8,128)(2,1)} %constant.14.clone.xh) | copy-start | bytes 614404
  35.4 55.0 %copy-start.6 = (bf16[160,160]{1,0:T(8,128)(2,1)S(1)}, bf16[160,160]{1,0:T(8,128)(2,1)}, u32[]{:S(2)}) copy-start(bf16[160,160]{1,0:T(8,128)(2,1)} %constant.17.clone.yl) | copy-start | bytes 153604
  35.4 55.0 %copy-start.7 = (bf16[160,160]{1,0:T(8,128)(2,1)S(1)}, bf16[160,160]{1,0:T(8,128)(2,1)}, u32[]{:S(2)}) copy-start(bf16[160,160]{1,0:T(8,128)(2,1)} %constant.16.clone.yh) | copy-start | bytes 153604
  53.1 58.4 %copy-start.1 = (f32[1,51200]{1,0:T(1,128)S(1)}, f32[1,51200]{1,0:T(1,128)}, u32[]{:S(2)}) copy-start(f32[1,51200]{1,0:T(1,128)} %param.13) | copy-start | bytes 614404
  93.4 18.1 %all-to-all-start.4 = ((f32[256,1,128]{2,1,0:T(1,128)}), f32[256,1,128]{2,1,0:T(1,128)S(1)}, u32[]{:S(2)}, u32[]{:S(2)}) async-start(f32[256,1,128]{2,1,0:T(1,128)} %bitcast.5), calls=%async_computation.4 | async-start | bytes 262144 | tf_op jit(solution)/shard_map/all_to_all | solution.py:265

commit v3 on v2

--- a/solution.py
+++ b/solution.py
@@ -168,21 +168,37 @@
                + jnp.dot(left_high, right_low, preferred_element_type=F32)))
 
 
-def first_kernel(c_ref, s_ref, x_hbm, y_hbm, cases_hbm, out_ref, back_ref, cases_ref, wide, tall, x_ref, y_ref, sems):
-    copies = [
-        pltpu.make_async_copy(y_hbm, y_ref, sems.at[0]),
-        pltpu.make_async_copy(x_hbm, x_ref, sems.at[1]),
-        pltpu.make_async_copy(cases_hbm, cases_ref, sems.at[2]),
-    ]
+def rows_of(flat, lines, grid):
+    for k in range(5):
+        lines[:, k * 128:(k + 1) * 128] = flat[pl.ds(k, 80, stride=5), :]
+    for k in range(4):
+        grid[k * 80:(k + 1) * 80, :] = lines[:, k * GY:(k + 1) * GY]
+
+
+def flat_of(grid, lines, flat):
+    for k in range(4):
+        lines[:, k * GY:(k + 1) * GY] = grid[k * 80:(k + 1) * 80, :]
+    for k in range(5):
+        flat[pl.ds(k, 80, stride=5), :] = lines[:, k * 128:(k + 1) * 128]
+
+
+def first_kernel(c_hbm, s_hbm, x_hbm, y_hbm, cases_hbm, out_ref, back_ref, cases_ref,
+                 wide, tall, lines, grid, c_ref, s_ref, x_ref, y_ref, sems):
+    pairs = ((c_hbm, c_ref), (s_hbm, s_ref), (y_hbm, y_ref), (x_hbm, x_ref), (cases_hbm, cases_ref))
+    copies = [pltpu.make_async_copy(*pair, sems.at[k]) for k, pair in enumerate(pairs)]
     for copy in copies:
         copy.start()
+    wide[:, PIECE:] = jnp.zeros((32, wide.shape[1] - PIECE), F32)
+    copies[0].wait()
     control = c_ref[...]
     back_ref[...] = 0.5 * jnp.sum(control * control, axis=(0, 1), keepdims=True)
-    coeffs = split2(control * s_ref[...])
-    wide[:, PIECE:] = jnp.zeros((32, wide.shape[1] - PIECE), F32)
-    copies[0].wait()
+    copies[1].wait()
+    c_ref[...] = control * s_ref[...]
+    rows_of(c_ref, lines, grid)
+    coeffs = split2(grid[...])
+    copies[2].wait()
     rows = split2(product(coeffs, (y_ref[0], y_ref[1])))
-    copies[1].wait()
+    copies[3].wait()
     field = product((x_ref[0], x_ref[1]), rows)
     for i in range(10):
         wide[:, i * GY:(i + 1) * GY] = field[i * 32:(i + 1) * 32]
@@ -191,7 +207,7 @@
     for r in range(BLOCKS, 16):
         tall[:, r, :] = jnp.zeros((32, 128), F32)
     out_ref[...] = tall[...].astype(BF16)
-    copies[2].wait()
+    copies[4].wait()
 
 
 def spread_kernel(in_ref, out_ref, tall, wide):
@@ -216,7 +232,8 @@
     out_ref[...] = tall[...].astype(BF16)
 
 
-def last_kernel(in_ref, c_ref, s_ref, xh, xl, yh, yl, back_ref, obs_ref, grad_ref, pay_ref, tall, wide, adj):
+def last_kernel(in_ref, c_ref, s_ref, xh, xl, yh, yl, back_ref, obs_ref, grad_ref, pay_ref,
+                tall, wide, adj, lines, grid):
     tall[...] = in_ref[...].astype(F32)
     for r in range(BLOCKS):
         wide[:, r * 128:(r + 1) * 128] = tall[:, r, :]
@@ -225,7 +242,9 @@
     part = adj[...]
     rows = (jnp.dot(xh[...], part, preferred_element_type=F32)
             + jnp.dot(xl[...], part, preferred_element_type=F32))
-    grad = c_ref[...] + s_ref[...] * product(split2(rows), (yh[...], yl[...]))
+    grid[...] = product(split2(rows), (yh[...], yl[...]))
+    flat_of(grid, lines, grad_ref)
+    grad = c_ref[...] + s_ref[...] * grad_ref[...]
     grad_ref[...] = grad
     cost = back_ref[...] + obs_ref[...]
     norm = jnp.sum(grad * grad, axis=(0, 1), keepdims=True)
@@ -266,22 +285,28 @@
 
 
 def per_device(control, spectrum, perturb, obs_index, innovation, obs_sigma, qc_class):
-    order = np.arange(GX).reshape(32, 10).T.reshape(-1)
-    table_x = lookup_table(GX)[:, order]
+    waves = np.arange(GX).reshape(80, 4).T.reshape(-1)
+    points = np.arange(GX).reshape(32, 10).T.reshape(-1)
+    table_x = lookup_table(GX)[waves][:, points]
     table_y = lookup_table(GY)
     cases = perturb.transpose(0, 2, 3, 1).reshape(2 * LEV, PIECE, MEMBERS)
-    control_grid = control.reshape(GX, GY)
-    spectrum_grid = spectrum.reshape(GX, GY)
+    control_flat = control.reshape(400, 128)
+    spectrum_flat = spectrum.reshape(400, 128)
     tall = pltpu.VMEM((32, 16, 128), F32)
     wide = pltpu.VMEM((32, BLOCKS * 128), F32)
-
+    lines = pltpu.VMEM((80, 640), F32)
+    grid = pltpu.VMEM((GX, GY), F32)
+    flat = pltpu.VMEM((400, 128), F32)
+
+    inputs = (control_flat, spectrum_flat, jnp.asarray(np.stack(two_parts(table_x.T))),
+              jnp.asarray(np.stack(two_parts(table_y))), cases)
     sent, back, cases = call(
         first_kernel,
         (((32, 16, 128), BF16), ((1, 1), F32), (cases.shape, BF16)),
-        [wide, tall, pltpu.VMEM((2, GX, GX), BF16), pltpu.VMEM((2, GY, GY), BF16),
-         pltpu.SemaphoreType.DMA((3,))],
-        "synthesis", specs=(2, 3, 4),
-    )(control_grid, spectrum_grid, np.stack(two_parts(table_x.T)), np.stack(two_parts(table_y)), cases)
+        [wide, tall, lines, grid, flat, flat, pltpu.VMEM((2, GX, GX), BF16),
+         pltpu.VMEM((2, GY, GY), BF16), pltpu.SemaphoreType.DMA((5,))],
+        "synthesis", specs=range(5),
+    )(*[pltpu.with_memory_space_constraint(value, pltpu.HBM) for value in inputs])
     pieces = exchanged(sent, SPACE)
     (copies,) = call(spread_kernel, (((8, 32, PIECE), BF16),), [tall, wide], "spread")(pieces)
     fields = exchanged(copies, TM).reshape(MEMBERS, PIECE)
@@ -291,14 +316,14 @@
     adjoint = exchanged(summed, SPACE)
     gradient, mine = call(
         last_kernel,
-        (((GX, GY), F32), ((MEMBERS, 128), F32)),
-        [tall, wide, pltpu.VMEM((GX, GY), BF16)],
+        (((400, 128), F32), ((MEMBERS, 128), F32)),
+        [tall, wide, pltpu.VMEM((GX, GY), BF16), lines, grid],
         "analysis",
-    )(adjoint, control_grid, spectrum_grid, *two_parts(table_x), *two_parts(table_y.T), back, obs)
+    )(adjoint, control_flat, spectrum_flat, *two_parts(table_x), *two_parts(table_y.T), back, obs)
     sums = exchanged(mine.reshape(MEMBERS, 1, 128), TM_SPACE).reshape(MEMBERS, 128)
     result, cost = call(
         step_kernel, (((400, 128), F32), ((1, 1), F32)), [], "step"
-    )(sums, control.reshape(400, 128), gradient.reshape(400, 128))
+    )(sums, control_flat, gradient)
     return result.reshape(1, GX * GY), cost.reshape(1)
 
 

time: 113 us -> 104 us (0.920)
  blocking collectives: 72.1 us -> 90 us
  waiting for transfers between devices: 12.6 us -> 0 us
  local copies, waits for them, and re-layouts: 6.84 us -> 0.05 us
  starting transfers between devices: 5.2 us -> 0 us
  other arithmetic: 2.06 us -> 0 us
    all_to_all x4 -> x5, blocking collectives: 72.1 us -> 90 us  [exchanged(): return lax.all_to_all(value, axis, split_axis=0, concat_axis=0, tiled=True)]
    all_to_all x1 -> x0, waiting for transfers between devices: 12.6 us -> none  [exchanged(): return lax.all_to_all(value, axis, split_axis=0, concat_axis=0, tiled=True)]
    unnamed x25 -> x20, local copies, waits for them, and re-layouts: 5.35 us -> 0.05 us
    all_to_all x1 -> x0, starting transfers between devices: 5.2 us -> none  [exchanged(): return lax.all_to_all(value, axis, split_axis=0, concat_axis=0, tiled=True)]
    unnamed x1 -> x0, other arithmetic: 2.06 us -> none
    reshape x3 -> x0, local copies, waits for them, and re-layouts: 1.49 us -> none  [the longest x1 1.08 us: per_device(): spectrum_grid = spectrum.reshape(GX, GY)]
  transfers between devices with their start and end apart: 1 -> 0, of which waited for: 1 -> 0; matrix products, arithmetic and copies ran while one was open for 0% -> 0% of each run, Pallas kernels for 0% -> 0%
where the time goes in v3:
time: 104 us
  blocking collectives  90 us (87%)
  Pallas kernels  13.4 us (13%)
    all_to_all x5, blocking collectives, exchanged(): return lax.all_to_all(value, axis, split_axis=0, concat_axis=0, tiled=True)  90 us
    pallas_call x5, Pallas kernels, run(): pl.pallas_call(kernel, out_shape=tuple((jax.ShapeDtypeStruct(*out) for ou...  7.74 us
    pallas_call x1, Pallas kernels, middle(): pl.pallas_call(middle_kernel, out_shape=(jax.ShapeDtypeStruct((256, PIECE...  5.7 us

profile of v3, /device:TPU:1, one launch (start us, length us, event | category | flops | bytes accessed | tf_op | source)
XLA Modules:
  0.0 104.2 jit_solution(15387277978411348322)
XLA Ops:
  0.6 0.0 copy-start.9
  0.6 0.0 copy-start.8
  0.7 0.0 copy-start.7
  0.7 0.0 copy-start.6
  0.7 3.9 %synthesis.1 = (bf16[32,16,128]{2,1,0:T(8,128)(2,1)S(1)}, f32[1,1]{1,0:T(1,128)}, bf16[8,1600,256]{2,1,0:T(8,128)(2,1)S(1)}) custom-call(f32[400,128]{1,0:T(8,128)} %bitcast.14, f32[400,128]{1,0:T(8,128)} %bitcast.18, bf16[2,320,320]{2,1,0:T(8,128)(2,1)} %constant.12.clone.x_hbm, bf16[2,160,160]{2,1,0:T(8,128)(2,1)} %constant.13.clone.y_hbm, ...), custom_call_target="tpu_custom_call" | custom-call | tf_op jit(solution)/shard_map/synthesis/pallas_call | solution.py:270
  4.6 23.4 %all_to_all.25.in_ref = bf16[32,16,128]{2,1,0:T(8,128)(2,1)S(1)} all-to-all(bf16[32,16,128]{2,1,0:T(8,128)(2,1)S(1)} %get-tuple-element.12), channel_id=1, replica_groups=mesh['tm_0'=2,'tm_1'=4,'space_0'=4,'space_1'=4,'space_2'=2] {'space_0','..., dimensions={0} | all-to-all | bytes 262144 | tf_op jit(solution)/shard_map/all_to_all | solution.py:284
  28.0 0.0 copy-start
  28.0 0.0 copy-start.1
  28.0 0.0 copy-start.2
  28.0 0.0 copy-start.3
  28.0 0.0 copy-start.4
  28.0 0.0 copy-start.5
  28.0 0.2 spread.1
  28.2 17.5 %all_to_all.26 = bf16[8,32,1600]{2,1,0:T(8,128)(2,1)S(1)} all-to-all(bf16[8,32,1600]{2,1,0:T(8,128)(2,1)S(1)} %spread.1), channel_id=1, replica_groups=mesh['tm_0'=2,'tm_1'=4,'space_0'=4,'space_1'=4,'space_2'=2] {'tm_0','tm_1'}, dimensions={0} | all-to-all | bytes 1638400 | tf_op jit(solution)/shard_map/all_to_all | solution.py:284
  45.7 0.0 copy-done.9
  45.7 0.0 copy-done.8
  45.7 0.0 copy-done.7
  45.7 0.0 copy-done.6
  45.7 5.7 %middle.1 = (bf16[256,1600]{1,0:T(8,128)(2,1)S(1)}, f32[1,1]{1,0:T(1,128)}) custom-call(bf16[8,1600,256]{2,1,0:T(8,128)(2,1)S(1)} %get-tuple-element.11.p_ref, bf16[256,1600]{1,0:T(8,128)(2,1)S(1)} %bitcast.13, s32[2,2048]{1,0:T(2,128)S(1)} %copy-done.6, f32[2,2048]{1,0:T(2,128)S(1)} %copy-done.7, f32[2,2048]{1,0:T(2,128)S(1)} %copy-done.8, ...), custom_call_target="tpu_custom_call" | custom-call | tf_op jit(solution)/shard_map/middle/pallas_call | solution.py:117
  51.4 14.9 %all_to_all.27.in_ref = bf16[8,32,1600]{2,1,0:T(8,128)(2,1)S(1)} all-to-all(bf16[8,32,1600]{2,1,0:T(8,128)(2,1)S(1)} %bitcast.17), channel_id=1, replica_groups=mesh['tm_0'=2,'tm_1'=4,'space_0'=4,'space_1'=4,'space_2'=2] {'tm_0','tm_1'}, dimensions={0} | all-to-all | bytes 1638400 | tf_op jit(solution)/shard_map/all_to_all | solution.py:284
  66.3 0.3 fold.1
  66.6 16.3 %all_to_all.28.in_ref = bf16[32,16,128]{2,1,0:T(8,128)(2,1)S(1)} all-to-all(bf16[32,16,128]{2,1,0:T(8,128)(2,1)S(1)} %fold.1), channel_id=1, replica_groups=mesh['tm_0'=2,'tm_1'=4,'space_0'=4,'space_1'=4,'space_2'=2] {'space_0','..., dimensions={0} | all-to-all | bytes 262144 | tf_op jit(solution)/shard_map/all_to_all | solution.py:284
  82.9 0.0 copy-done
  82.9 0.0 copy-done.1
  82.9 0.0 copy-done.2
  82.9 0.0 copy-done.3
  82.9 0.0 copy-done.4
  82.9 0.0 copy-done.5
  83.0 2.5 %analysis.1 = (f32[400,128]{1,0:T(8,128)S(1)}, f32[256,128]{1,0:T(8,128)S(1)}) custom-call(bf16[32,16,128]{2,1,0:T(8,128)(2,1)S(1)} %all_to_all.28.in_ref, f32[400,128]{1,0:T(8,128)S(1)} %bitcast.15, f32[400,128]{1,0:T(8,128)S(1)} %bitcast.19, bf16[320,320]{1,0:T(8,128)(2,1)S(1)} %copy-done.3, bf16[320,320]{1,0:T(8,128)(2,1)S(1)} %copy-done.2, ...), custom_call_target="tpu_custom_call" | custom-call | tf_op jit(solution)/shard_map/analysis/pallas_call | solution.py:270
  85.5 17.9 %all_to_all.29 = f32[256,1,128]{2,1,0:T(1,128)S(1)} all-to-all(f32[256,1,128]{2,1,0:T(1,128)S(1)} %bitcast.21), channel_id=1, replica_groups=mesh['tm_0'=2,'tm_1'=4,'space_0'=4,'space_1'=4,'space_2'=2] {'tm_0','tm_..., dimensions={0} | all-to-all | bytes 262144 | tf_op jit(solution)/shard_map/all_to_all | solution.py:284
  103.4 0.9 step.1
Async XLA Ops:
  0.6 45.0 %copy-start.9 = (s32[2,2048]{1,0:T(2,128)S(1)}, s32[2,2048]{1,0:T(2,128)}, u32[]{:S(2)}) copy-start(s32[2,2048]{1,0:T(2,128)} %qc_ref.1) | copy-start | bytes 49156
  0.6 45.0 %copy-start.8 = (f32[2,2048]{1,0:T(2,128)S(1)}, f32[2,2048]{1,0:T(2,128)}, u32[]{:S(2)}) copy-start(f32[2,2048]{1,0:T(2,128)} %sig_ref.1) | copy-start | bytes 49156
  0.7 45.0 %copy-start.7 = (f32[2,2048]{1,0:T(2,128)S(1)}, f32[2,2048]{1,0:T(2,128)}, u32[]{:S(2)}) copy-start(f32[2,2048]{1,0:T(2,128)} %inn_ref.1) | copy-start | bytes 49156
  0.7 45.0 %copy-start.6 = (s32[2,2048]{1,0:T(2,128)S(1)}, s32[2,2048]{1,0:T(2,128)}, u32[]{:S(2)}) copy-start(s32[2,2048]{1,0:T(2,128)} %idx_ref.1) | copy-start | bytes 49156
  28.0 55.0 %copy-start = (f32[1,51200]{1,0:T(1,128)S(1)}, f32[1,51200]{1,0:T(1,128)}, u32[]{:S(2)}) copy-start(f32[1,51200]{1,0:T(1,128)} %param.13) | copy-start | bytes 614404
  28.0 55.0 %copy-start.1 = (f32[51200]{0:T(1024)S(1)}, f32[51200]{0:T(1024)}, u32[]{:S(2)}) copy-start(f32[51200]{0:T(1024)} %param.14) | copy-start | bytes 614404
  28.0 55.0 %copy-start.2 = (bf16[320,320]{1,0:T(8,128)(2,1)S(1)}, bf16[320,320]{1,0:T(8,128)(2,1)}, u32[]{:S(2)}) copy-start(bf16[320,320]{1,0:T(8,128)(2,1)} %constant.15.clone.xl) | copy-start | bytes 614404
  28.0 55.0 %copy-start.3 = (bf16[320,320]{1,0:T(8,128)(2,1)S(1)}, bf16[320,320]{1,0:T(8,128)(2,1)}, u32[]{:S(2)}) copy-start(bf16[320,320]{1,0:T(8,128)(2,1)} %constant.14.clone.xh) | copy-start | bytes 614404
  28.0 55.0 %copy-start.4 = (bf16[160,160]{1,0:T(8,128)(2,1)S(1)}, bf16[160,160]{1,0:T(8,128)(2,1)}, u32[]{:S(2)}) copy-start(bf16[160,160]{1,0:T(8,128)(2,1)} %constant.17.clone.yl) | copy-start | bytes 153604
  28.0 55.0 %copy-start.5 = (bf16[160,160]{1,0:T(8,128)(2,1)S(1)}, bf16[160,160]{1,0:T(8,128)(2,1)}, u32[]{:S(2)}) copy-start(bf16[160,160]{1,0:T(8,128)(2,1)} %constant.16.clone.yh) | copy-start | bytes 153604

commit v4 on v3

--- a/solution.py
+++ b/solution.py
@@ -14,6 +14,7 @@
 ROWS = 64
 OBS = 2048
 CHUNK = 256
+EARLY = 1024
 
 
 def split3(value):
@@ -24,13 +25,18 @@
     return first, second, third
 
 
-def middle_kernel(p_ref, f_ref, idx_ref, inn_ref, sig_ref, qc_ref, adj_ref, cost_ref,
-                  cells, table, modelled, grads, where_row, where_lane):
+def middle_kernel(early_ref, cases_hbm, f_ref, idx_ref, inn_ref, sig_ref, qc_ref, adj_ref, cost_ref,
+                  late_ref, cells, table, modelled, grads, where_row, where_lane, sem):
     f32 = jnp.float32
+    copy = pltpu.make_async_copy(cases_hbm.at[:, EARLY:, :], late_ref, sem)
+    copy.start()
     cells[...] = jnp.zeros_like(cells)
 
     def forward(blk, start, width):
-        rows = p_ref[:, start:start + width, :].reshape(8 * width, 256)
+        if start < EARLY:
+            rows = early_ref[:, start:start + width, :].reshape(8 * width, 256)
+        else:
+            rows = late_ref[:, start - EARLY:start - EARLY + width, :].reshape(8 * width, 256)
         prod = jnp.dot(rows, f_ref[:, start:start + width], preferred_element_type=f32)
         same = lax.broadcasted_iota(jnp.int32, (width, width), 0) == lax.broadcasted_iota(
             jnp.int32, (width, width), 1)
@@ -41,6 +47,8 @@
             cells[k // LEV, at:at + 1, 0:width] = row
 
     for blk in range(BLOCKS):
+        if blk * 128 == EARLY:
+            copy.wait()
         forward(blk, blk * 128, min(128, PIECE - blk * 128))
 
     index = idx_ref[...]
@@ -73,7 +81,7 @@
     scaled = (modelled[...] - inn_ref[...]) / sigma
     scaled_sq = scaled * scaled / radius_sq
     terms = 0.5 * radius_sq * jnp.log1p(scaled_sq)
-    cost_ref[...] = jnp.sum(terms, axis=(0, 1), keepdims=True)
+    cost_ref[...] = jnp.broadcast_to(jnp.sum(terms, axis=(0, 1), keepdims=True), (8, 128))
     grad = scaled / ((1.0 + scaled_sq) * sigma)
     first, second, third = split3(grad)
     grads[0] = first.astype(f32)
@@ -100,37 +108,42 @@
         start = blk * 128
         width = min(128, PIECE - start)
         halves = []
+        cols = pltpu.roll(columns, (128 - blk) % 128, axis=1)
         for half in range(width // 64):
             lanes = slice(half * 64, half * 64 + 64)
-            points = slice(start + half * 64, start + half * 64 + 64)
+            first = start + half * 64
+            held, first = (early_ref, first) if start < EARLY else (late_ref, first - EARLY)
             total = jnp.zeros((64, 256), f32)
             for k in range(8):
-                j = k // LEV * ROWS + k % LEV * BLOCKS + blk
-                total = total + p_ref[k, points, :].astype(f32) * columns[lanes, j:j + 1]
+                j = k // LEV * ROWS + k % LEV * BLOCKS
+                total = total + held[k, first:first + 64, :].astype(f32) * cols[lanes, j:j + 1]
             halves.append(total)
         total = jnp.concatenate(halves, axis=0)
         adj_ref[:, start:start + width] = jnp.transpose(total).astype(jnp.bfloat16)
 
 
-def middle(cases, fields, obs_index, innovation, obs_sigma, qc_class):
+def middle(early, cases, fields, obs_index, innovation, obs_sigma, qc_class):
     vm = pl.BlockSpec(memory_space=pltpu.VMEM)
     return pl.pallas_call(
         middle_kernel,
         out_shape=(jax.ShapeDtypeStruct((256, PIECE), jnp.bfloat16),
-                   jax.ShapeDtypeStruct((1, 1), jnp.float32)),
-        in_specs=[vm] * 6,
+                   jax.ShapeDtypeStruct((8, 128), jnp.float32)),
+        in_specs=[vm, pl.BlockSpec(memory_space=pltpu.HBM)] + [vm] * 5,
         out_specs=(vm, vm),
         scratch_shapes=[
+            pltpu.VMEM((8, PIECE - EARLY, 256), jnp.bfloat16),
             pltpu.VMEM((2, ROWS, 128), jnp.float32),
             pltpu.VMEM((2, 128, 3 * ROWS), jnp.bfloat16),
             pltpu.VMEM((2, OBS), jnp.float32),
             pltpu.VMEM((3, 2, OBS), jnp.float32),
             pltpu.VMEM((2, OBS), jnp.int32),
             pltpu.VMEM((2, OBS), jnp.int32),
+            pltpu.SemaphoreType.DMA,
         ],
         compiler_params=pltpu.CompilerParams(vmem_limit_bytes=40 * 1024 * 1024),
         name="middle",
-    )(cases, fields, obs_index, innovation, obs_sigma, qc_class)
+    )(early, pltpu.with_memory_space_constraint(cases, pltpu.HBM), fields, obs_index, innovation,
+      obs_sigma, qc_class)
 
 
 F32 = jnp.float32
@@ -182,16 +195,17 @@
         flat[pl.ds(k, 80, stride=5), :] = lines[:, k * 128:(k + 1) * 128]
 
 
-def first_kernel(c_hbm, s_hbm, x_hbm, y_hbm, cases_hbm, out_ref, back_ref, cases_ref,
+def first_kernel(c_hbm, s_hbm, x_hbm, y_hbm, cases_hbm, out_ref, back_ref, early_ref,
                  wide, tall, lines, grid, c_ref, s_ref, x_ref, y_ref, sems):
-    pairs = ((c_hbm, c_ref), (s_hbm, s_ref), (y_hbm, y_ref), (x_hbm, x_ref), (cases_hbm, cases_ref))
+    pairs = ((c_hbm, c_ref), (s_hbm, s_ref), (y_hbm, y_ref), (x_hbm, x_ref), (cases_hbm.at[:, 0:EARLY, :], early_ref))
     copies = [pltpu.make_async_copy(*pair, sems.at[k]) for k, pair in enumerate(pairs)]
     for copy in copies:
         copy.start()
     wide[:, PIECE:] = jnp.zeros((32, wide.shape[1] - PIECE), F32)
     copies[0].wait()
     control = c_ref[...]
-    back_ref[...] = 0.5 * jnp.sum(control * control, axis=(0, 1), keepdims=True)
+    back = 0.5 * jnp.sum(control * control, axis=(0, 1), keepdims=True)
+    back_ref[...] = jnp.broadcast_to(back, (8, 128))
     copies[1].wait()
     c_ref[...] = control * s_ref[...]
     rows_of(c_ref, lines, grid)
@@ -246,7 +260,7 @@
     flat_of(grid, lines, grad_ref)
     grad = c_ref[...] + s_ref[...] * grad_ref[...]
     grad_ref[...] = grad
-    cost = back_ref[...] + obs_ref[...]
+    cost = back_ref[0:1, 0:1] + obs_ref[0:1, 0:1]
     norm = jnp.sum(grad * grad, axis=(0, 1), keepdims=True)
     lane = lax.broadcasted_iota(jnp.int32, (MEMBERS, 128), 1)
     pay_ref[...] = jnp.where(lane == 0, cost, jnp.where(lane == 1, norm, 0.0))
@@ -300,9 +314,9 @@
 
     inputs = (control_flat, spectrum_flat, jnp.asarray(np.stack(two_parts(table_x.T))),
               jnp.asarray(np.stack(two_parts(table_y))), cases)
-    sent, back, cases = call(
+    sent, back, early = call(
         first_kernel,
-        (((32, 16, 128), BF16), ((1, 1), F32), (cases.shape, BF16)),
+        (((32, 16, 128), BF16), ((8, 128), F32), ((2 * LEV, EARLY, MEMBERS), BF16)),
         [wide, tall, lines, grid, flat, flat, pltpu.VMEM((2, GX, GX), BF16),
          pltpu.VMEM((2, GY, GY), BF16), pltpu.SemaphoreType.DMA((5,))],
         "synthesis", specs=range(5),
@@ -310,7 +324,7 @@
     pieces = exchanged(sent, SPACE)
     (copies,) = call(spread_kernel, (((8, 32, PIECE), BF16),), [tall, wide], "spread")(pieces)
     fields = exchanged(copies, TM).reshape(MEMBERS, PIECE)
-    partial, obs = middle(cases, fields, obs_index, innovation, obs_sigma, qc_class)
+    partial, obs = middle(early, cases, fields, obs_index, innovation, obs_sigma, qc_class)
     terms = exchanged(partial.reshape(8, 32, PIECE), TM)
     (summed,) = call(fold_kernel, (((32, 16, 128), BF16),), [tall, wide], "fold")(terms)
     adjoint = exchanged(summed, SPACE)

time: 104 us -> 102 us (0.981)
  Pallas kernels: 13.4 us -> 11.2 us
    pallas_call x5, Pallas kernels: 7.74 us -> 5.25 us  [run(): pl.pallas_call(kernel, out_shape=tuple((jax.ShapeDtypeStruct(*out) for ou...]
where the time goes in v4:
time: 102 us
  blocking collectives  89.9 us (88%)
  Pallas kernels  11.2 us (11%)
    all_to_all x5, blocking collectives, exchanged(): return lax.all_to_all(value, axis, split_axis=0, concat_axis=0, tiled=True)  89.9 us
    pallas_call x1, Pallas kernels, middle(): pl.pallas_call(middle_kernel, out_shape=(jax.ShapeDtypeStruct((256, PIECE...  5.92 us
    pallas_call x5, Pallas kernels, run(): pl.pallas_call(kernel, out_shape=tuple((jax.ShapeDtypeStruct(*out) for ou...  5.25 us

profile of v4, /device:TPU:1, one launch (start us, length us, event | category | flops | bytes accessed | tf_op | source)
XLA Modules:
  0.0 101.9 jit_solution(17609577705153936432)
XLA Ops:
  0.6 0.0 copy-start.9
  0.6 0.0 copy-start.8
  0.7 0.0 copy-start.7
  0.7 0.0 copy-start.6
  0.7 2.7 %synthesis.1 = (bf16[32,16,128]{2,1,0:T(8,128)(2,1)S(1)}, f32[8,128]{1,0:T(8,128)S(1)}, bf16[8,1024,256]{2,1,0:T(8,128)(2,1)S(1)}) custom-call(f32[400,128]{1,0:T(8,128)} %bitcast.14, f32[400,128]{1,0:T(8,128)} %bitcast.18, bf16[2,320,320]{2,1,0:T(8,128)(2,1)} %constant.12.clone.x_hbm, bf16[2,160,160]{2,1,0:T(8,128)(2,1)} %constant.13.clone.y_hbm, ...), custom_call_target="tpu_custom_call" | custom-call | tf_op jit(solution)/shard_map/synthesis/pallas_call | solution.py:284
  3.4 23.4 %all_to_all.25.in_ref = bf16[32,16,128]{2,1,0:T(8,128)(2,1)S(1)} all-to-all(bf16[32,16,128]{2,1,0:T(8,128)(2,1)S(1)} %get-tuple-element.12), channel_id=1, replica_groups=mesh['tm_0'=2,'tm_1'=4,'space_0'=4,'space_1'=4,'space_2'=2] {'space_0','..., dimensions={0} | all-to-all | bytes 262144 | tf_op jit(solution)/shard_map/all_to_all | solution.py:298
  26.8 0.2 spread.1
  26.9 17.4 %all_to_all.26 = bf16[8,32,1600]{2,1,0:T(8,128)(2,1)S(1)} all-to-all(bf16[8,32,1600]{2,1,0:T(8,128)(2,1)S(1)} %spread.1), channel_id=1, replica_groups=mesh['tm_0'=2,'tm_1'=4,'space_0'=4,'space_1'=4,'space_2'=2] {'tm_0','tm_1'}, dimensions={0} | all-to-all | bytes 1638400 | tf_op jit(solution)/shard_map/all_to_all | solution.py:298
  44.3 0.0 copy-done.9
  44.3 0.0 copy-done.8
  44.3 0.0 copy-done.7
  44.3 0.0 copy-done.6
  44.3 0.0 copy-start
  44.3 0.0 copy-start.1
  44.3 0.0 copy-start.2
  44.4 0.0 copy-start.3
  44.4 0.0 copy-start.4
  44.4 0.0 copy-start.5
  44.4 5.9 %middle.1 = (bf16[256,1600]{1,0:T(8,128)(2,1)S(1)}, f32[8,128]{1,0:T(8,128)S(1)}) custom-call(bf16[8,1024,256]{2,1,0:T(8,128)(2,1)S(1)} %get-tuple-element.11.early_ref, bf16[8,1600,256]{2,1,0:T(8,128)(2,1)} %bitcast.23, bf16[256,1600]{1,0:T(8,128)(2,1)S(1)} %bitcast.13, s32[2,2048]{1,0:T(2,128)S(1)} %copy-done.6, f32[2,2048]{1,0:T(2,128)S(1)} %copy-done.7, ...), custom_call_target="tpu_custom_call" | custom-call | tf_op jit(solution)/shard_map/middle/pallas_call | solution.py:127
  50.3 14.9 %all_to_all.27.in_ref = bf16[8,32,1600]{2,1,0:T(8,128)(2,1)S(1)} all-to-all(bf16[8,32,1600]{2,1,0:T(8,128)(2,1)S(1)} %bitcast.17), channel_id=1, replica_groups=mesh['tm_0'=2,'tm_1'=4,'space_0'=4,'space_1'=4,'space_2'=2] {'tm_0','tm_1'}, dimensions={0} | all-to-all | bytes 1638400 | tf_op jit(solution)/shard_map/all_to_all | solution.py:298
  65.3 0.3 fold.1
  65.6 16.3 %all_to_all.28.in_ref = bf16[32,16,128]{2,1,0:T(8,128)(2,1)S(1)} all-to-all(bf16[32,16,128]{2,1,0:T(8,128)(2,1)S(1)} %fold.1), channel_id=1, replica_groups=mesh['tm_0'=2,'tm_1'=4,'space_0'=4,'space_1'=4,'space_2'=2] {'space_0','..., dimensions={0} | all-to-all | bytes 262144 | tf_op jit(solution)/shard_map/all_to_all | solution.py:298
  81.9 0.0 copy-done
  81.9 0.0 copy-done.1
  81.9 0.0 copy-done.2
  81.9 0.0 copy-done.3
  81.9 0.0 copy-done.4
  81.9 0.0 copy-done.5
  81.9 1.2 %analysis.1 = (f32[400,128]{1,0:T(8,128)S(1)}, f32[256,128]{1,0:T(8,128)S(1)}) custom-call(bf16[32,16,128]{2,1,0:T(8,128)(2,1)S(1)} %all_to_all.28.in_ref, f32[400,128]{1,0:T(8,128)S(1)} %bitcast.15, f32[400,128]{1,0:T(8,128)S(1)} %bitcast.19, bf16[320,320]{1,0:T(8,128)(2,1)S(1)} %copy-done.3, bf16[320,320]{1,0:T(8,128)(2,1)S(1)} %copy-done.2, ...), custom_call_target="tpu_custom_call" | custom-call | tf_op jit(solution)/shard_map/analysis/pallas_call | solution.py:284
  83.2 17.9 %all_to_all.29 = f32[256,1,128]{2,1,0:T(1,128)S(1)} all-to-all(f32[256,1,128]{2,1,0:T(1,128)S(1)} %bitcast.21), channel_id=1, replica_groups=mesh['tm_0'=2,'tm_1'=4,'space_0'=4,'space_1'=4,'space_2'=2] {'tm_0','tm_..., dimensions={0} | all-to-all | bytes 262144 | tf_op jit(solution)/shard_map/all_to_all | solution.py:298
  101.0 0.9 step.1
Async XLA Ops:
  0.6 43.7 %copy-start.9 = (s32[2,2048]{1,0:T(2,128)S(1)}, s32[2,2048]{1,0:T(2,128)}, u32[]{:S(2)}) copy-start(s32[2,2048]{1,0:T(2,128)} %qc_ref.1) | copy-start | bytes 49156
  0.6 43.7 %copy-start.8 = (f32[2,2048]{1,0:T(2,128)S(1)}, f32[2,2048]{1,0:T(2,128)}, u32[]{:S(2)}) copy-start(f32[2,2048]{1,0:T(2,128)} %sig_ref.1) | copy-start | bytes 49156
  0.7 43.7 %copy-start.7 = (f32[2,2048]{1,0:T(2,128)S(1)}, f32[2,2048]{1,0:T(2,128)}, u32[]{:S(2)}) copy-start(f32[2,2048]{1,0:T(2,128)} %inn_ref.1) | copy-start | bytes 49156
  0.7 43.7 %copy-start.6 = (s32[2,2048]{1,0:T(2,128)S(1)}, s32[2,2048]{1,0:T(2,128)}, u32[]{:S(2)}) copy-start(s32[2,2048]{1,0:T(2,128)} %idx_ref.1) | copy-start | bytes 49156
  44.3 37.6 %copy-start = (f32[1,51200]{1,0:T(1,128)S(1)}, f32[1,51200]{1,0:T(1,128)}, u32[]{:S(2)}) copy-start(f32[1,51200]{1,0:T(1,128)} %param.13) | copy-start | bytes 614404
  44.3 37.6 %copy-start.1 = (f32[51200]{0:T(1024)S(1)}, f32[51200]{0:T(1024)}, u32[]{:S(2)}) copy-start(f32[51200]{0:T(1024)} %param.14) | copy-start | bytes 614404
  44.3 37.5 %copy-start.2 = (bf16[320,320]{1,0:T(8,128)(2,1)S(1)}, bf16[320,320]{1,0:T(8,128)(2,1)}, u32[]{:S(2)}) copy-start(bf16[320,320]{1,0:T(8,128)(2,1)} %constant.15.clone.xl) | copy-start | bytes 614404
  44.4 37.5 %copy-start.3 = (bf16[320,320]{1,0:T(8,128)(2,1)S(1)}, bf16[320,320]{1,0:T(8,128)(2,1)}, u32[]{:S(2)}) copy-start(bf16[320,320]{1,0:T(8,128)(2,1)} %constant.14.clone.xh) | copy-start | bytes 614404
  44.4 37.5 %copy-start.4 = (bf16[160,160]{1,0:T(8,128)(2,1)S(1)}, bf16[160,160]{1,0:T(8,128)(2,1)}, u32[]{:S(2)}) copy-start(bf16[160,160]{1,0:T(8,128)(2,1)} %constant.17.clone.yl) | copy-start | bytes 153604
  44.4 37.5 %copy-start.5 = (bf16[160,160]{1,0:T(8,128)(2,1)S(1)}, bf16[160,160]{1,0:T(8,128)(2,1)}, u32[]{:S(2)}) copy-start(bf16[160,160]{1,0:T(8,128)(2,1)} %constant.16.clone.yh) | copy-start | bytes 153604

commit v5 on v4

--- a/solution.py
+++ b/solution.py
@@ -14,7 +14,7 @@
 ROWS = 64
 OBS = 2048
 CHUNK = 256
-EARLY = 1024
+EARLY = 1280
 
 
 def split3(value):
@@ -103,22 +103,33 @@
         sums.append(total[0:ROWS] + total[ROWS:2 * ROWS] + total[2 * ROWS:3 * ROWS])
     update = jnp.concatenate(sums, axis=0).astype(jnp.bfloat16).astype(f32)
     columns = jnp.transpose(update)
+    same = lax.broadcasted_iota(jnp.int32, (128, 128), 0) == lax.broadcasted_iota(
+        jnp.int32, (128, 128), 1)
 
     for blk in range(BLOCKS):
         start = blk * 128
         width = min(128, PIECE - start)
-        halves = []
-        cols = pltpu.roll(columns, (128 - blk) % 128, axis=1)
-        for half in range(width // 64):
-            lanes = slice(half * 64, half * 64 + 64)
-            first = start + half * 64
-            held, first = (early_ref, first) if start < EARLY else (late_ref, first - EARLY)
-            total = jnp.zeros((64, 256), f32)
+        held, first = (early_ref, start) if start < EARLY else (late_ref, start - EARLY)
+        if blk % 3 != 0 and width == 128:
+            diagonals = []
             for k in range(8):
-                j = k // LEV * ROWS + k % LEV * BLOCKS
-                total = total + held[k, first:first + 64, :].astype(f32) * cols[lanes, j:j + 1]
-            halves.append(total)
-        total = jnp.concatenate(halves, axis=0)
+                j = k // LEV * ROWS + k % LEV * BLOCKS + blk
+                diagonals.append(jnp.where(same, update[j:j + 1], 0.0).astype(jnp.bfloat16))
+            total = jnp.dot(jnp.concatenate(diagonals, axis=1),
+                            held[:, first:first + width, :].reshape(8 * width, 256),
+                            preferred_element_type=f32)
+        else:
+            cols = pltpu.roll(columns, (128 - blk) % 128, axis=1)
+            halves = []
+            for half in range(width // 64):
+                lanes = slice(half * 64, half * 64 + 64)
+                here = first + half * 64
+                total = jnp.zeros((64, 256), f32)
+                for k in range(8):
+                    j = k // LEV * ROWS + k % LEV * BLOCKS
+                    total = total + held[k, here:here + 64, :].astype(f32) * cols[lanes, j:j + 1]
+                halves.append(total)
+            total = jnp.concatenate(halves, axis=0)
         adj_ref[:, start:start + width] = jnp.transpose(total).astype(jnp.bfloat16)
 
 

time: 102 us -> 101 us (level)
  Pallas kernels: 11.2 us -> 10.1 us
    pallas_call x1, Pallas kernels: 5.92 us -> 4.53 us  [middle(): pl.pallas_call(middle_kernel, out_shape=(jax.ShapeDtypeStruct((256, PIECE...]
where the time goes in v5:
time: 101 us
  blocking collectives  89.9 us (89%)
  Pallas kernels  10.1 us (10%)
    all_to_all x5, blocking collectives, exchanged(): return lax.all_to_all(value, axis, split_axis=0, concat_axis=0, tiled=True)  89.9 us
    pallas_call x5, Pallas kernels, run(): pl.pallas_call(kernel, out_shape=tuple((jax.ShapeDtypeStruct(*out) for ou...  5.56 us
    pallas_call x1, Pallas kernels, middle(): pl.pallas_call(middle_kernel, out_shape=(jax.ShapeDtypeStruct((256, PIECE...  4.53 us

profile of v5, /device:TPU:1, one launch (start us, length us, event | category | flops | bytes accessed | tf_op | source)
XLA Modules:
  0.0 100.8 jit_solution(2531754523991665365)
XLA Ops:
  0.6 0.0 copy-start.9
  0.6 0.0 copy-start.8
  0.7 0.0 copy-start.7
  0.7 0.0 copy-start.6
  0.7 3.0 %synthesis.1 = (bf16[32,16,128]{2,1,0:T(8,128)(2,1)S(1)}, f32[8,128]{1,0:T(8,128)S(1)}, bf16[8,1280,256]{2,1,0:T(8,128)(2,1)S(1)}) custom-call(f32[400,128]{1,0:T(8,128)} %bitcast.14, f32[400,128]{1,0:T(8,128)} %bitcast.18, bf16[2,320,320]{2,1,0:T(8,128)(2,1)} %constant.12.clone.x_hbm, bf16[2,160,160]{2,1,0:T(8,128)(2,1)} %constant.13.clone.y_hbm, ...), custom_call_target="tpu_custom_call" | custom-call | tf_op jit(solution)/shard_map/synthesis/pallas_call | solution.py:295
  3.7 23.4 %all_to_all.25.in_ref = bf16[32,16,128]{2,1,0:T(8,128)(2,1)S(1)} all-to-all(bf16[32,16,128]{2,1,0:T(8,128)(2,1)S(1)} %get-tuple-element.12), channel_id=1, replica_groups=mesh['tm_0'=2,'tm_1'=4,'space_0'=4,'space_1'=4,'space_2'=2] {'space_0','..., dimensions={0} | all-to-all | bytes 262144 | tf_op jit(solution)/shard_map/all_to_all | solution.py:309
  27.1 0.2 spread.1
  27.2 17.4 %all_to_all.26 = bf16[8,32,1600]{2,1,0:T(8,128)(2,1)S(1)} all-to-all(bf16[8,32,1600]{2,1,0:T(8,128)(2,1)S(1)} %spread.1), channel_id=1, replica_groups=mesh['tm_0'=2,'tm_1'=4,'space_0'=4,'space_1'=4,'space_2'=2] {'tm_0','tm_1'}, dimensions={0} | all-to-all | bytes 1638400 | tf_op jit(solution)/shard_map/all_to_all | solution.py:309
  44.6 0.0 copy-done.9
  44.6 0.0 copy-done.8
  44.6 0.0 copy-done.7
  44.6 0.0 copy-done.6
  44.6 0.0 copy-start
  44.6 0.0 copy-start.1
  44.7 0.0 copy-start.2
  44.7 0.0 copy-start.3
  44.7 0.0 copy-start.4
  44.7 0.0 copy-start.5
  44.7 4.5 %middle.1 = (bf16[256,1600]{1,0:T(8,128)(2,1)S(1)}, f32[8,128]{1,0:T(8,128)S(1)}) custom-call(bf16[8,1280,256]{2,1,0:T(8,128)(2,1)S(1)} %get-tuple-element.11.early_ref, bf16[8,1600,256]{2,1,0:T(8,128)(2,1)} %bitcast.23, bf16[256,1600]{1,0:T(8,128)(2,1)S(1)} %bitcast.13, s32[2,2048]{1,0:T(2,128)S(1)} %copy-done.6, f32[2,2048]{1,0:T(2,128)S(1)} %copy-done.7, ...), custom_call_target="tpu_custom_call" | custom-call | tf_op jit(solution)/shard_map/middle/pallas_call | solution.py:138
  49.2 14.9 %all_to_all.27.in_ref = bf16[8,32,1600]{2,1,0:T(8,128)(2,1)S(1)} all-to-all(bf16[8,32,1600]{2,1,0:T(8,128)(2,1)S(1)} %bitcast.17), channel_id=1, replica_groups=mesh['tm_0'=2,'tm_1'=4,'space_0'=4,'space_1'=4,'space_2'=2] {'tm_0','tm_1'}, dimensions={0} | all-to-all | bytes 1638400 | tf_op jit(solution)/shard_map/all_to_all | solution.py:309
  64.2 0.3 fold.1
  64.5 16.3 %all_to_all.28.in_ref = bf16[32,16,128]{2,1,0:T(8,128)(2,1)S(1)} all-to-all(bf16[32,16,128]{2,1,0:T(8,128)(2,1)S(1)} %fold.1), channel_id=1, replica_groups=mesh['tm_0'=2,'tm_1'=4,'space_0'=4,'space_1'=4,'space_2'=2] {'space_0','..., dimensions={0} | all-to-all | bytes 262144 | tf_op jit(solution)/shard_map/all_to_all | solution.py:309
  80.8 0.0 copy-done
  80.8 0.0 copy-done.1
  80.8 0.0 copy-done.2
  80.8 0.0 copy-done.3
  80.8 0.0 copy-done.4
  80.8 0.0 copy-done.5
  80.8 1.2 %analysis.1 = (f32[400,128]{1,0:T(8,128)S(1)}, f32[256,128]{1,0:T(8,128)S(1)}) custom-call(bf16[32,16,128]{2,1,0:T(8,128)(2,1)S(1)} %all_to_all.28.in_ref, f32[400,128]{1,0:T(8,128)S(1)} %bitcast.15, f32[400,128]{1,0:T(8,128)S(1)} %bitcast.19, bf16[320,320]{1,0:T(8,128)(2,1)S(1)} %copy-done.3, bf16[320,320]{1,0:T(8,128)(2,1)S(1)} %copy-done.2, ...), custom_call_target="tpu_custom_call" | custom-call | tf_op jit(solution)/shard_map/analysis/pallas_call | solution.py:295
  82.1 17.9 %all_to_all.29 = f32[256,1,128]{2,1,0:T(1,128)S(1)} all-to-all(f32[256,1,128]{2,1,0:T(1,128)S(1)} %bitcast.21), channel_id=1, replica_groups=mesh['tm_0'=2,'tm_1'=4,'space_0'=4,'space_1'=4,'space_2'=2] {'tm_0','tm_..., dimensions={0} | all-to-all | bytes 262144 | tf_op jit(solution)/shard_map/all_to_all | solution.py:309
  99.9 0.9 step.1
Async XLA Ops:
  0.6 44.0 %copy-start.9 = (s32[2,2048]{1,0:T(2,128)S(1)}, s32[2,2048]{1,0:T(2,128)}, u32[]{:S(2)}) copy-start(s32[2,2048]{1,0:T(2,128)} %qc_ref.1) | copy-start | bytes 49156
  0.6 44.0 %copy-start.8 = (f32[2,2048]{1,0:T(2,128)S(1)}, f32[2,2048]{1,0:T(2,128)}, u32[]{:S(2)}) copy-start(f32[2,2048]{1,0:T(2,128)} %sig_ref.1) | copy-start | bytes 49156
  0.7 44.0 %copy-start.7 = (f32[2,2048]{1,0:T(2,128)S(1)}, f32[2,2048]{1,0:T(2,128)}, u32[]{:S(2)}) copy-start(f32[2,2048]{1,0:T(2,128)} %inn_ref.1) | copy-start | bytes 49156
  0.7 44.0 %copy-start.6 = (s32[2,2048]{1,0:T(2,128)S(1)}, s32[2,2048]{1,0:T(2,128)}, u32[]{:S(2)}) copy-start(s32[2,2048]{1,0:T(2,128)} %idx_ref.1) | copy-start | bytes 49156
  44.6 36.2 %copy-start = (f32[1,51200]{1,0:T(1,128)S(1)}, f32[1,51200]{1,0:T(1,128)}, u32[]{:S(2)}) copy-start(f32[1,51200]{1,0:T(1,128)} %param.13) | copy-start | bytes 614404
  44.6 36.2 %copy-start.1 = (f32[51200]{0:T(1024)S(1)}, f32[51200]{0:T(1024)}, u32[]{:S(2)}) copy-start(f32[51200]{0:T(1024)} %param.14) | copy-start | bytes 614404
  44.7 36.1 %copy-start.2 = (bf16[320,320]{1,0:T(8,128)(2,1)S(1)}, bf16[320,320]{1,0:T(8,128)(2,1)}, u32[]{:S(2)}) copy-start(bf16[320,320]{1,0:T(8,128)(2,1)} %constant.15.clone.xl) | copy-start | bytes 614404
  44.7 36.1 %copy-start.3 = (bf16[320,320]{1,0:T(8,128)(2,1)S(1)}, bf16[320,320]{1,0:T(8,128)(2,1)}, u32[]{:S(2)}) copy-start(bf16[320,320]{1,0:T(8,128)(2,1)} %constant.14.clone.xh) | copy-start | bytes 614404
  44.7 36.1 %copy-start.4 = (bf16[160,160]{1,0:T(8,128)(2,1)S(1)}, bf16[160,160]{1,0:T(8,128)(2,1)}, u32[]{:S(2)}) copy-start(bf16[160,160]{1,0:T(8,128)(2,1)} %constant.17.clone.yl) | copy-start | bytes 153604
  44.7 36.1 %copy-start.5 = (bf16[160,160]{1,0:T(8,128)(2,1)S(1)}, bf16[160,160]{1,0:T(8,128)(2,1)}, u32[]{:S(2)}) copy-start(bf16[160,160]{1,0:T(8,128)(2,1)} %constant.16.clone.yh) | copy-start | bytes 153604

commit v6 on v5

--- a/solution.py
+++ b/solution.py
@@ -37,7 +37,13 @@
             rows = early_ref[:, start:start + width, :].reshape(8 * width, 256)
         else:
             rows = late_ref[:, start - EARLY:start - EARLY + width, :].reshape(8 * width, 256)
-        prod = jnp.dot(rows, f_ref[:, start:start + width], preferred_element_type=f32)
+        if width == 128:
+            fields = f_ref[:, blk * 32:(blk + 1) * 32, :].reshape(256, 128)
+        else:
+            tail = f_ref[:, 384:400, :].astype(f32)
+            tail = jnp.concatenate([tail, pltpu.roll(tail, 64, axis=2)], axis=1)
+            fields = tail.reshape(256, 128)[:, 0:64].astype(jnp.bfloat16)
+        prod = jnp.dot(rows, fields, preferred_element_type=f32)
         same = lax.broadcasted_iota(jnp.int32, (width, width), 0) == lax.broadcasted_iota(
             jnp.int32, (width, width), 1)
         for k in range(8):
@@ -130,14 +136,20 @@
                     total = total + held[k, here:here + 64, :].astype(f32) * cols[lanes, j:j + 1]
                 halves.append(total)
             total = jnp.concatenate(halves, axis=0)
-        adj_ref[:, start:start + width] = jnp.transpose(total).astype(jnp.bfloat16)
+        total = jnp.transpose(total)
+        if width == 128:
+            adj_ref[:, blk * 32:(blk + 1) * 32, :] = total.astype(jnp.bfloat16).reshape(8, 32, 128)
+        else:
+            total = total.reshape(8, 32, 64)
+            total = jnp.concatenate([total[:, 0:16], total[:, 16:32]], axis=2)
+            adj_ref[:, 384:400, :] = total.astype(jnp.bfloat16)
 
 
 def middle(early, cases, fields, obs_index, innovation, obs_sigma, qc_class):
     vm = pl.BlockSpec(memory_space=pltpu.VMEM)
     return pl.pallas_call(
         middle_kernel,
-        out_shape=(jax.ShapeDtypeStruct((256, PIECE), jnp.bfloat16),
+        out_shape=(jax.ShapeDtypeStruct((8, 400, 128), jnp.bfloat16),
                    jax.ShapeDtypeStruct((8, 128), jnp.float32)),
         in_specs=[vm, pl.BlockSpec(memory_space=pltpu.HBM)] + [vm] * 5,
         out_specs=(vm, vm),
@@ -235,23 +247,26 @@
     copies[4].wait()
 
 
-def spread_kernel(in_ref, out_ref, tall, wide):
+def spread_kernel(in_ref, out_ref, tall, lines):
     tall[...] = in_ref[...].astype(F32)
-    for r in range(BLOCKS):
-        wide[:, r * 128:(r + 1) * 128] = tall[:, r, :]
-    value = wide[:, 0:PIECE].astype(BF16)
+    for r in range(12):
+        lines[r * 32:(r + 1) * 32, :] = tall[:, r, :]
+    tail = tall[:, 12, :]
+    lane = lax.broadcasted_iota(jnp.int32, (16, 128), 1)
+    lines[384:400, :] = jnp.where(lane < 64, tail[0:16], pltpu.roll(tail[16:32], 64, axis=1))
+    value = lines[...].astype(BF16)
     for k in range(8):
         out_ref[k] = value
 
 
-def fold_kernel(in_ref, out_ref, tall, wide):
+def fold_kernel(in_ref, out_ref, tall):
     total = in_ref[0].astype(F32)
     for k in range(1, 8):
         total = total + in_ref[k].astype(F32)
-    wide[:, 0:PIECE] = total
-    wide[:, PIECE:] = jnp.zeros((32, wide.shape[1] - PIECE), F32)
-    for r in range(BLOCKS):
-        tall[:, r, :] = wide[:, r * 128:(r + 1) * 128]
+    for r in range(12):
+        tall[:, r, :] = total[r * 32:(r + 1) * 32]
+    tail = total[384:400]
+    tall[:, 12, :] = jnp.concatenate([tail, pltpu.roll(tail, 64, axis=1)], axis=0)
     for r in range(BLOCKS, 16):
         tall[:, r, :] = jnp.zeros((32, 128), F32)
     out_ref[...] = tall[...].astype(BF16)
@@ -333,11 +348,11 @@
         "synthesis", specs=range(5),
     )(*[pltpu.with_memory_space_constraint(value, pltpu.HBM) for value in inputs])
     pieces = exchanged(sent, SPACE)
-    (copies,) = call(spread_kernel, (((8, 32, PIECE), BF16),), [tall, wide], "spread")(pieces)
-    fields = exchanged(copies, TM).reshape(MEMBERS, PIECE)
+    (copies,) = call(spread_kernel, (((8, 400, 128), BF16),), [tall, flat], "spread")(pieces)
+    fields = exchanged(copies, TM)
     partial, obs = middle(early, cases, fields, obs_index, innovation, obs_sigma, qc_class)
-    terms = exchanged(partial.reshape(8, 32, PIECE), TM)
-    (summed,) = call(fold_kernel, (((32, 16, 128), BF16),), [tall, wide], "fold")(terms)
+    terms = exchanged(partial, TM)
+    (summed,) = call(fold_kernel, (((32, 16, 128), BF16),), [tall], "fold")(terms)
     adjoint = exchanged(summed, SPACE)
     gradient, mine = call(
         last_kernel,

time: 101 us -> 100 us (0.990)
  no operation moved by 1% of the time
where the time goes in v6:
time: 100 us
  blocking collectives  89.2 us (89%)
  Pallas kernels  10 us (10%)
    all_to_all x5, blocking collectives, exchanged(): return lax.all_to_all(value, axis, split_axis=0, concat_axis=0, tiled=True)  89.2 us
    pallas_call x5, Pallas kernels, run(): pl.pallas_call(kernel, out_shape=tuple((jax.ShapeDtypeStruct(*out) for ou...  5.57 us
    pallas_call x1, Pallas kernels, middle(): pl.pallas_call(middle_kernel, out_shape=(jax.ShapeDtypeStruct((8, 400, 12...  4.45 us

profile of v6, /device:TPU:1, one launch (start us, length us, event | category | flops | bytes accessed | tf_op | source)
XLA Modules:
  0.0 100.0 jit_solution(16143739964876971109)
XLA Ops:
  0.6 0.0 copy-start.9
  0.6 0.0 copy-start.8
  0.7 0.0 copy-start.7
  0.7 0.0 copy-start.6
  0.7 3.0 %synthesis.1 = (bf16[32,16,128]{2,1,0:T(8,128)(2,1)S(1)}, f32[8,128]{1,0:T(8,128)S(1)}, bf16[8,1280,256]{2,1,0:T(8,128)(2,1)S(1)}) custom-call(f32[400,128]{1,0:T(8,128)} %bitcast.11, f32[400,128]{1,0:T(8,128)} %bitcast.14, bf16[2,320,320]{2,1,0:T(8,128)(2,1)} %constant.12.clone.x_hbm, bf16[2,160,160]{2,1,0:T(8,128)(2,1)} %constant.13.clone.y_hbm, ...), custom_call_target="tpu_custom_call" | custom-call | tf_op jit(solution)/shard_map/synthesis/pallas_call | solution.py:310
  3.7 23.4 %all_to_all.25.in_ref = bf16[32,16,128]{2,1,0:T(8,128)(2,1)S(1)} all-to-all(bf16[32,16,128]{2,1,0:T(8,128)(2,1)S(1)} %get-tuple-element.12), channel_id=1, replica_groups=mesh['tm_0'=2,'tm_1'=4,'space_0'=4,'space_1'=4,'space_2'=2] {'space_0','..., dimensions={0} | all-to-all | bytes 262144 | tf_op jit(solution)/shard_map/all_to_all | solution.py:324
  27.1 0.2 spread.1
  27.3 17.2 %all_to_all.26.f_ref = bf16[8,400,128]{2,1,0:T(8,128)(2,1)S(1)} all-to-all(bf16[8,400,128]{2,1,0:T(8,128)(2,1)S(1)} %spread.1), channel_id=1, replica_groups=mesh['tm_0'=2,'tm_1'=4,'space_0'=4,'space_1'=4,'space_2'=2] {'tm_0','tm_1'}, dimensions={0} | all-to-all | bytes 1638400 | tf_op jit(solution)/shard_map/all_to_all | solution.py:324
  44.5 0.0 copy-done.9
  44.5 0.0 copy-done.8
  44.5 0.0 copy-done.7
  44.5 0.0 copy-done.6
  44.5 0.0 copy-start
  44.5 0.0 copy-start.1
  44.5 0.0 copy-start.2
  44.5 0.0 copy-start.3
  44.5 0.0 copy-start.4
  44.5 0.0 copy-start.5
  44.6 4.5 %middle.1 = (bf16[8,400,128]{2,1,0:T(8,128)(2,1)S(1)}, f32[8,128]{1,0:T(8,128)S(1)}) custom-call(bf16[8,1280,256]{2,1,0:T(8,128)(2,1)S(1)} %get-tuple-element.11.early_ref, bf16[8,1600,256]{2,1,0:T(8,128)(2,1)} %bitcast.19, bf16[8,400,128]{2,1,0:T(8,128)(2,1)S(1)} %all_to_all.26.f_ref, s32[2,2048]{1,0:T(2,128)S(1)} %copy-done.6, f32[2,2048]{1,0:T(2,128)S(1)} %copy-done.7, ...), custom_call_target="tpu_custom_call" | custom-call | tf_op jit(solution)/shard_map/middle/pallas_call | solution.py:150
  49.0 14.7 %all_to_all.27.in_ref = bf16[8,400,128]{2,1,0:T(8,128)(2,1)S(1)} all-to-all(bf16[8,400,128]{2,1,0:T(8,128)(2,1)S(1)} %get-tuple-element.13), channel_id=1, replica_groups=mesh['tm_0'=2,'tm_1'=4,'space_0'=4,'space_1'=4,'space_2'=2] {'tm_0','tm_1'}, dimensions={0} | all-to-all | bytes 1638400 | tf_op jit(solution)/shard_map/all_to_all | solution.py:324
  63.7 0.3 fold.1
  64.0 16.0 %all_to_all.28.in_ref = bf16[32,16,128]{2,1,0:T(8,128)(2,1)S(1)} all-to-all(bf16[32,16,128]{2,1,0:T(8,128)(2,1)S(1)} %fold.1), channel_id=1, replica_groups=mesh['tm_0'=2,'tm_1'=4,'space_0'=4,'space_1'=4,'space_2'=2] {'space_0','..., dimensions={0} | all-to-all | bytes 262144 | tf_op jit(solution)/shard_map/all_to_all | solution.py:324
  80.0 0.0 copy-done
  80.0 0.0 copy-done.1
  80.0 0.0 copy-done.2
  80.0 0.0 copy-done.3
  80.1 0.0 copy-done.4
  80.1 0.0 copy-done.5
  80.1 1.2 %analysis.1 = (f32[400,128]{1,0:T(8,128)S(1)}, f32[256,128]{1,0:T(8,128)S(1)}) custom-call(bf16[32,16,128]{2,1,0:T(8,128)(2,1)S(1)} %all_to_all.28.in_ref, f32[400,128]{1,0:T(8,128)S(1)} %bitcast.12, f32[400,128]{1,0:T(8,128)S(1)} %bitcast.15, bf16[320,320]{1,0:T(8,128)(2,1)S(1)} %copy-done.3, bf16[320,320]{1,0:T(8,128)(2,1)S(1)} %copy-done.2, ...), custom_call_target="tpu_custom_call" | custom-call | tf_op jit(solution)/shard_map/analysis/pallas_call | solution.py:310
  81.3 17.9 %all_to_all.29 = f32[256,1,128]{2,1,0:T(1,128)S(1)} all-to-all(f32[256,1,128]{2,1,0:T(1,128)S(1)} %bitcast.17), channel_id=1, replica_groups=mesh['tm_0'=2,'tm_1'=4,'space_0'=4,'space_1'=4,'space_2'=2] {'tm_0','tm_..., dimensions={0} | all-to-all | bytes 262144 | tf_op jit(solution)/shard_map/all_to_all | solution.py:324
  99.2 0.9 step.1
Async XLA Ops:
  0.6 43.8 %copy-start.9 = (s32[2,2048]{1,0:T(2,128)S(1)}, s32[2,2048]{1,0:T(2,128)}, u32[]{:S(2)}) copy-start(s32[2,2048]{1,0:T(2,128)} %qc_ref.1) | copy-start | bytes 49156
  0.6 43.8 %copy-start.8 = (f32[2,2048]{1,0:T(2,128)S(1)}, f32[2,2048]{1,0:T(2,128)}, u32[]{:S(2)}) copy-start(f32[2,2048]{1,0:T(2,128)} %sig_ref.1) | copy-start | bytes 49156
  0.7 43.8 %copy-start.7 = (f32[2,2048]{1,0:T(2,128)S(1)}, f32[2,2048]{1,0:T(2,128)}, u32[]{:S(2)}) copy-start(f32[2,2048]{1,0:T(2,128)} %inn_ref.1) | copy-start | bytes 49156
  0.7 43.8 %copy-start.6 = (s32[2,2048]{1,0:T(2,128)S(1)}, s32[2,2048]{1,0:T(2,128)}, u32[]{:S(2)}) copy-start(s32[2,2048]{1,0:T(2,128)} %idx_ref.1) | copy-start | bytes 49156
  44.5 35.6 %copy-start = (f32[1,51200]{1,0:T(1,128)S(1)}, f32[1,51200]{1,0:T(1,128)}, u32[]{:S(2)}) copy-start(f32[1,51200]{1,0:T(1,128)} %param.13) | copy-start | bytes 614404
  44.5 35.5 %copy-start.1 = (f32[51200]{0:T(1024)S(1)}, f32[51200]{0:T(1024)}, u32[]{:S(2)}) copy-start(f32[51200]{0:T(1024)} %param.14) | copy-start | bytes 614404
  44.5 35.5 %copy-start.2 = (bf16[320,320]{1,0:T(8,128)(2,1)S(1)}, bf16[320,320]{1,0:T(8,128)(2,1)}, u32[]{:S(2)}) copy-start(bf16[320,320]{1,0:T(8,128)(2,1)} %constant.15.clone.xl) | copy-start | bytes 614404
  44.5 35.5 %copy-start.3 = (bf16[320,320]{1,0:T(8,128)(2,1)S(1)}, bf16[320,320]{1,0:T(8,128)(2,1)}, u32[]{:S(2)}) copy-start(bf16[320,320]{1,0:T(8,128)(2,1)} %constant.14.clone.xh) | copy-start | bytes 614404
  44.5 35.5 %copy-start.4 = (bf16[160,160]{1,0:T(8,128)(2,1)S(1)}, bf16[160,160]{1,0:T(8,128)(2,1)}, u32[]{:S(2)}) copy-start(bf16[160,160]{1,0:T(8,128)(2,1)} %constant.17.clone.yl) | copy-start | bytes 153604
  44.5 35.5 %copy-start.5 = (bf16[160,160]{1,0:T(8,128)(2,1)S(1)}, bf16[160,160]{1,0:T(8,128)(2,1)}, u32[]{:S(2)}) copy-start(bf16[160,160]{1,0:T(8,128)(2,1)} %constant.16.clone.yh) | copy-start | bytes 153604

commit v7 on v6

--- a/solution.py
+++ b/solution.py
@@ -1,3 +1,5 @@
+import functools
+
 import jax
 import jax.numpy as jnp
 import ml_dtypes
@@ -15,6 +17,7 @@
 OBS = 2048
 CHUNK = 256
 EARLY = 1280
+VECTOR = (1,4,7,10,)
 
 
 def split3(value):
@@ -26,7 +29,7 @@
 
 
 def middle_kernel(early_ref, cases_hbm, f_ref, idx_ref, inn_ref, sig_ref, qc_ref, adj_ref, cost_ref,
-                  late_ref, cells, table, modelled, grads, where_row, where_lane, sem):
+                  late_ref, sums_by_lane, cells, table, modelled, grads, where_row, where_lane, sem):
     f32 = jnp.float32
     copy = pltpu.make_async_copy(cases_hbm.at[:, EARLY:, :], late_ref, sem)
     copy.start()
@@ -43,6 +46,13 @@
             tail = f_ref[:, 384:400, :].astype(f32)
             tail = jnp.concatenate([tail, pltpu.roll(tail, 64, axis=2)], axis=1)
             fields = tail.reshape(256, 128)[:, 0:64].astype(jnp.bfloat16)
+        if blk in VECTOR:
+            members = jnp.transpose(fields.astype(f32))
+            for k in range(8):
+                terms = rows[k * width:(k + 1) * width].astype(f32) * members
+                at = k % LEV * BLOCKS + blk
+                sums_by_lane[k // LEV, :, at:at + 1] = jnp.sum(terms, axis=1, keepdims=True)
+            return
         prod = jnp.dot(rows, fields, preferred_element_type=f32)
         same = lax.broadcasted_iota(jnp.int32, (width, width), 0) == lax.broadcasted_iota(
             jnp.int32, (width, width), 1)
@@ -65,7 +75,10 @@
     where_lane[...] = point & 127
 
     for t in range(2):
-        parts = split3(jnp.transpose(cells[t]))
+        column = lax.broadcasted_iota(jnp.int32, (128, ROWS), 1)
+        summed = functools.reduce(jnp.logical_or, [
+            column == level * BLOCKS + blk for level in range(LEV) for blk in VECTOR])
+        parts = split3(jnp.where(summed, sums_by_lane[t], jnp.transpose(cells[t])))
         for k in range(3):
             table[t, :, k * ROWS:(k + 1) * ROWS] = parts[k]
 
@@ -155,6 +168,7 @@
         out_specs=(vm, vm),
         scratch_shapes=[
             pltpu.VMEM((8, PIECE - EARLY, 256), jnp.bfloat16),
+            pltpu.VMEM((2, 128, ROWS), jnp.float32),
             pltpu.VMEM((2, ROWS, 128), jnp.float32),
             pltpu.VMEM((2, 128, 3 * ROWS), jnp.bfloat16),
             pltpu.VMEM((2, OBS), jnp.float32),

time: 100 us -> 100 us (level)
  no operation moved by 1% of the time
where the time goes in v7:
time: 100 us
  blocking collectives  89.2 us (89%)
  Pallas kernels  9.97 us (10%)
    all_to_all x5, blocking collectives, exchanged(): return lax.all_to_all(value, axis, split_axis=0, concat_axis=0, tiled=True)  89.2 us
    pallas_call x5, Pallas kernels, run(): pl.pallas_call(kernel, out_shape=tuple((jax.ShapeDtypeStruct(*out) for ou...  5.57 us
    pallas_call x1, Pallas kernels, middle(): pl.pallas_call(middle_kernel, out_shape=(jax.ShapeDtypeStruct((8, 400, 12...  4.4 us

profile of v7, /device:TPU:1, one launch (start us, length us, event | category | flops | bytes accessed | tf_op | source)
XLA Modules:
  0.0 100.0 jit_solution(10104572319068577113)
XLA Ops:
  0.6 0.0 copy-start.9
  0.6 0.0 copy-start.8
  0.7 0.0 copy-start.7
  0.7 0.0 copy-start.6
  0.7 3.0 %synthesis.1 = (bf16[32,16,128]{2,1,0:T(8,128)(2,1)S(1)}, f32[8,128]{1,0:T(8,128)S(1)}, bf16[8,1280,256]{2,1,0:T(8,128)(2,1)S(1)}) custom-call(f32[400,128]{1,0:T(8,128)} %bitcast.11, f32[400,128]{1,0:T(8,128)} %bitcast.14, bf16[2,320,320]{2,1,0:T(8,128)(2,1)} %constant.12.clone.x_hbm, bf16[2,160,160]{2,1,0:T(8,128)(2,1)} %constant.13.clone.y_hbm, ...), custom_call_target="tpu_custom_call" | custom-call | tf_op jit(solution)/shard_map/synthesis/pallas_call | solution.py:324
  3.7 23.4 %all_to_all.25.in_ref = bf16[32,16,128]{2,1,0:T(8,128)(2,1)S(1)} all-to-all(bf16[32,16,128]{2,1,0:T(8,128)(2,1)S(1)} %get-tuple-element.12), channel_id=1, replica_groups=mesh['tm_0'=2,'tm_1'=4,'space_0'=4,'space_1'=4,'space_2'=2] {'space_0','..., dimensions={0} | all-to-all | bytes 262144 | tf_op jit(solution)/shard_map/all_to_all | solution.py:338
  27.1 0.2 spread.1
  27.3 17.2 %all_to_all.26.f_ref = bf16[8,400,128]{2,1,0:T(8,128)(2,1)S(1)} all-to-all(bf16[8,400,128]{2,1,0:T(8,128)(2,1)S(1)} %spread.1), channel_id=1, replica_groups=mesh['tm_0'=2,'tm_1'=4,'space_0'=4,'space_1'=4,'space_2'=2] {'tm_0','tm_1'}, dimensions={0} | all-to-all | bytes 1638400 | tf_op jit(solution)/shard_map/all_to_all | solution.py:338
  44.5 0.0 copy-done.9
  44.5 0.0 copy-done.8
  44.5 0.0 copy-done.7
  44.5 0.0 copy-done.6
  44.5 0.0 copy-start
  44.5 0.0 copy-start.1
  44.5 0.0 copy-start.2
  44.5 0.0 copy-start.3
  44.5 0.0 copy-start.4
  44.5 0.0 copy-start.5
  44.6 4.4 %middle.1 = (bf16[8,400,128]{2,1,0:T(8,128)(2,1)S(1)}, f32[8,128]{1,0:T(8,128)S(1)}) custom-call(bf16[8,1280,256]{2,1,0:T(8,128)(2,1)S(1)} %get-tuple-element.11.early_ref, bf16[8,1600,256]{2,1,0:T(8,128)(2,1)} %bitcast.19, bf16[8,400,128]{2,1,0:T(8,128)(2,1)S(1)} %all_to_all.26.f_ref, s32[2,2048]{1,0:T(2,128)S(1)} %copy-done.6, f32[2,2048]{1,0:T(2,128)S(1)} %copy-done.7, ...), custom_call_target="tpu_custom_call" | custom-call | tf_op jit(solution)/shard_map/middle/pallas_call | solution.py:163
  49.0 14.7 %all_to_all.27.in_ref = bf16[8,400,128]{2,1,0:T(8,128)(2,1)S(1)} all-to-all(bf16[8,400,128]{2,1,0:T(8,128)(2,1)S(1)} %get-tuple-element.13), channel_id=1, replica_groups=mesh['tm_0'=2,'tm_1'=4,'space_0'=4,'space_1'=4,'space_2'=2] {'tm_0','tm_1'}, dimensions={0} | all-to-all | bytes 1638400 | tf_op jit(solution)/shard_map/all_to_all | solution.py:338
  63.7 0.3 fold.1
  64.0 16.0 %all_to_all.28.in_ref = bf16[32,16,128]{2,1,0:T(8,128)(2,1)S(1)} all-to-all(bf16[32,16,128]{2,1,0:T(8,128)(2,1)S(1)} %fold.1), channel_id=1, replica_groups=mesh['tm_0'=2,'tm_1'=4,'space_0'=4,'space_1'=4,'space_2'=2] {'space_0','..., dimensions={0} | all-to-all | bytes 262144 | tf_op jit(solution)/shard_map/all_to_all | solution.py:338
  80.0 0.0 copy-done
  80.0 0.0 copy-done.1
  80.0 0.0 copy-done.2
  80.0 0.0 copy-done.3
  80.0 0.0 copy-done.4
  80.0 0.0 copy-done.5
  80.0 1.2 %analysis.1 = (f32[400,128]{1,0:T(8,128)S(1)}, f32[256,128]{1,0:T(8,128)S(1)}) custom-call(bf16[32,16,128]{2,1,0:T(8,128)(2,1)S(1)} %all_to_all.28.in_ref, f32[400,128]{1,0:T(8,128)S(1)} %bitcast.12, f32[400,128]{1,0:T(8,128)S(1)} %bitcast.15, bf16[320,320]{1,0:T(8,128)(2,1)S(1)} %copy-done.3, bf16[320,320]{1,0:T(8,128)(2,1)S(1)} %copy-done.2, ...), custom_call_target="tpu_custom_call" | custom-call | tf_op jit(solution)/shard_map/analysis/pallas_call | solution.py:324
  81.3 17.9 %all_to_all.29 = f32[256,1,128]{2,1,0:T(1,128)S(1)} all-to-all(f32[256,1,128]{2,1,0:T(1,128)S(1)} %bitcast.17), channel_id=1, replica_groups=mesh['tm_0'=2,'tm_1'=4,'space_0'=4,'space_1'=4,'space_2'=2] {'tm_0','tm_..., dimensions={0} | all-to-all | bytes 262144 | tf_op jit(solution)/shard_map/all_to_all | solution.py:338
  99.1 0.9 step.1
Async XLA Ops:
  0.6 43.8 %copy-start.9 = (s32[2,2048]{1,0:T(2,128)S(1)}, s32[2,2048]{1,0:T(2,128)}, u32[]{:S(2)}) copy-start(s32[2,2048]{1,0:T(2,128)} %qc_ref.1) | copy-start | bytes 49156
  0.6 43.8 %copy-start.8 = (f32[2,2048]{1,0:T(2,128)S(1)}, f32[2,2048]{1,0:T(2,128)}, u32[]{:S(2)}) copy-start(f32[2,2048]{1,0:T(2,128)} %sig_ref.1) | copy-start | bytes 49156
  0.7 43.8 %copy-start.7 = (f32[2,2048]{1,0:T(2,128)S(1)}, f32[2,2048]{1,0:T(2,128)}, u32[]{:S(2)}) copy-start(f32[2,2048]{1,0:T(2,128)} %inn_ref.1) | copy-start | bytes 49156
  0.7 43.8 %copy-start.6 = (s32[2,2048]{1,0:T(2,128)S(1)}, s32[2,2048]{1,0:T(2,128)}, u32[]{:S(2)}) copy-start(s32[2,2048]{1,0:T(2,128)} %idx_ref.1) | copy-start | bytes 49156
  44.5 35.5 %copy-start = (f32[1,51200]{1,0:T(1,128)S(1)}, f32[1,51200]{1,0:T(1,128)}, u32[]{:S(2)}) copy-start(f32[1,51200]{1,0:T(1,128)} %param.13) | copy-start | bytes 614404
  44.5 35.5 %copy-start.1 = (f32[51200]{0:T(1024)S(1)}, f32[51200]{0:T(1024)}, u32[]{:S(2)}) copy-start(f32[51200]{0:T(1024)} %param.14) | copy-start | bytes 614404
  44.5 35.5 %copy-start.2 = (bf16[320,320]{1,0:T(8,128)(2,1)S(1)}, bf16[320,320]{1,0:T(8,128)(2,1)}, u32[]{:S(2)}) copy-start(bf16[320,320]{1,0:T(8,128)(2,1)} %constant.15.clone.xl) | copy-start | bytes 614404
  44.5 35.5 %copy-start.3 = (bf16[320,320]{1,0:T(8,128)(2,1)S(1)}, bf16[320,320]{1,0:T(8,128)(2,1)}, u32[]{:S(2)}) copy-start(bf16[320,320]{1,0:T(8,128)(2,1)} %constant.14.clone.xh) | copy-start | bytes 614404
  44.5 35.5 %copy-start.4 = (bf16[160,160]{1,0:T(8,128)(2,1)S(1)}, bf16[160,160]{1,0:T(8,128)(2,1)}, u32[]{:S(2)}) copy-start(bf16[160,160]{1,0:T(8,128)(2,1)} %constant.17.clone.yl) | copy-start | bytes 153604
  44.5 35.5 %copy-start.5 = (bf16[160,160]{1,0:T(8,128)(2,1)S(1)}, bf16[160,160]{1,0:T(8,128)(2,1)}, u32[]{:S(2)}) copy-start(bf16[160,160]{1,0:T(8,128)(2,1)} %constant.16.clone.yh) | copy-start | bytes 153604

commit v8 on v7

--- a/solution.py
+++ b/solution.py
@@ -28,8 +28,13 @@
     return first, second, third
 
 
-def middle_kernel(early_ref, cases_hbm, f_ref, idx_ref, inn_ref, sig_ref, qc_ref, adj_ref, cost_ref,
-                  late_ref, sums_by_lane, cells, table, modelled, grads, where_row, where_lane, sem):
+def level_of(index):
+    return ((index >= PIECE).astype(jnp.int32) + (index >= 2 * PIECE).astype(jnp.int32)
+            + (index >= 3 * PIECE).astype(jnp.int32))
+
+
+def middle_kernel(early_ref, cases_hbm, f_ref, row_hot, lane_hot, idx_ref, inn_ref, sig_ref, qc_ref, adj_ref, cost_ref,
+                  late_ref, sums_by_lane, cells, table, modelled, grads, where_lane, sem):
     f32 = jnp.float32
     copy = pltpu.make_async_copy(cases_hbm.at[:, EARLY:, :], late_ref, sem)
     copy.start()
@@ -68,11 +73,7 @@
         forward(blk, blk * 128, min(128, PIECE - blk * 128))
 
     index = idx_ref[...]
-    level = ((index >= PIECE).astype(jnp.int32) + (index >= 2 * PIECE).astype(jnp.int32)
-             + (index >= 3 * PIECE).astype(jnp.int32))
-    point = index - level * PIECE
-    where_row[...] = level * BLOCKS + (point >> 7)
-    where_lane[...] = point & 127
+    where_lane[...] = (index - level_of(index) * PIECE) & 127
 
     for t in range(2):
         column = lax.broadcasted_iota(jnp.int32, (128, ROWS), 1)
@@ -82,13 +83,12 @@
         for k in range(3):
             table[t, :, k * ROWS:(k + 1) * ROWS] = parts[k]
 
-    row_id = lax.broadcasted_iota(jnp.int32, (ROWS, CHUNK), 0)
     lane_id = lax.broadcasted_iota(jnp.int32, (128, CHUNK), 0)
 
     for t in range(2):
         for c in range(OBS // CHUNK):
             at = slice(c * CHUNK, (c + 1) * CHUNK)
-            hot = jnp.where(row_id == where_row[t:t + 1, at], 1.0, 0.0).astype(jnp.bfloat16)
+            hot = row_hot[t, :, at]
             hot = jnp.concatenate([hot, hot, hot], axis=0)
             lines = jnp.dot(table[t], hot, preferred_element_type=f32)
             lines = jnp.where(lane_id == where_lane[t:t + 1, at], lines, 0.0)
@@ -112,11 +112,10 @@
         total = jnp.zeros((3 * ROWS, 128), f32)
         for c in range(OBS // CHUNK):
             at = slice(c * CHUNK, (c + 1) * CHUNK)
-            hot = row_id == where_row[t:t + 1, at]
+            hot = row_hot[t, :, at]
             left = jnp.concatenate(
-                [jnp.where(hot, grads[k, t:t + 1, at], 0.0).astype(jnp.bfloat16) for k in range(3)],
-                axis=0)
-            right = jnp.where(lane_id == where_lane[t:t + 1, at], 1.0, 0.0).astype(jnp.bfloat16)
+                [hot * grads[k, t:t + 1, at].astype(jnp.bfloat16) for k in range(3)], axis=0)
+            right = lane_hot[t, :, at]
             total = total + lax.dot_general(left, right, (((1,), (1,)), ((), ())),
                                             preferred_element_type=f32)
         sums.append(total[0:ROWS] + total[ROWS:2 * ROWS] + total[2 * ROWS:3 * ROWS])
@@ -158,13 +157,13 @@
             adj_ref[:, 384:400, :] = total.astype(jnp.bfloat16)
 
 
-def middle(early, cases, fields, obs_index, innovation, obs_sigma, qc_class):
+def middle(early, cases, fields, row_hot, lane_hot, obs_index, innovation, obs_sigma, qc_class):
     vm = pl.BlockSpec(memory_space=pltpu.VMEM)
     return pl.pallas_call(
         middle_kernel,
         out_shape=(jax.ShapeDtypeStruct((8, 400, 128), jnp.bfloat16),
                    jax.ShapeDtypeStruct((8, 128), jnp.float32)),
-        in_specs=[vm, pl.BlockSpec(memory_space=pltpu.HBM)] + [vm] * 5,
+        in_specs=[vm, pl.BlockSpec(memory_space=pltpu.HBM)] + [vm] * 7,
         out_specs=(vm, vm),
         scratch_shapes=[
             pltpu.VMEM((8, PIECE - EARLY, 256), jnp.bfloat16),
@@ -174,12 +173,11 @@
             pltpu.VMEM((2, OBS), jnp.float32),
             pltpu.VMEM((3, 2, OBS), jnp.float32),
             pltpu.VMEM((2, OBS), jnp.int32),
-            pltpu.VMEM((2, OBS), jnp.int32),
             pltpu.SemaphoreType.DMA,
         ],
         compiler_params=pltpu.CompilerParams(vmem_limit_bytes=40 * 1024 * 1024),
         name="middle",
-    )(early, pltpu.with_memory_space_constraint(cases, pltpu.HBM), fields, obs_index, innovation,
+    )(early, pltpu.with_memory_space_constraint(cases, pltpu.HBM), fields, row_hot, lane_hot, obs_index, innovation,
       obs_sigma, qc_class)
 
 
@@ -232,9 +230,10 @@
         flat[pl.ds(k, 80, stride=5), :] = lines[:, k * 128:(k + 1) * 128]
 
 
-def first_kernel(c_hbm, s_hbm, x_hbm, y_hbm, cases_hbm, out_ref, back_ref, early_ref,
-                 wide, tall, lines, grid, c_ref, s_ref, x_ref, y_ref, sems):
-    pairs = ((c_hbm, c_ref), (s_hbm, s_ref), (y_hbm, y_ref), (x_hbm, x_ref), (cases_hbm.at[:, 0:EARLY, :], early_ref))
+def first_kernel(c_hbm, s_hbm, x_hbm, y_hbm, cases_hbm, idx_hbm, out_ref, back_ref, early_ref, row_hot, lane_hot,
+                 wide, tall, lines, grid, c_ref, s_ref, x_ref, y_ref, idx_ref, sems):
+    pairs = ((c_hbm, c_ref), (s_hbm, s_ref), (y_hbm, y_ref), (x_hbm, x_ref), (idx_hbm, idx_ref),
+             (cases_hbm.at[:, 0:EARLY, :], early_ref))
     copies = [pltpu.make_async_copy(*pair, sems.at[k]) for k, pair in enumerate(pairs)]
     for copy in copies:
         copy.start()
@@ -259,6 +258,17 @@
         tall[:, r, :] = jnp.zeros((32, 128), F32)
     out_ref[...] = tall[...].astype(BF16)
     copies[4].wait()
+    index = idx_ref[...]
+    level = level_of(index)
+    point = index - level * PIECE
+    row = level * BLOCKS + (point >> 7)
+    lane = point & 127
+    row_id = lax.broadcasted_iota(jnp.int32, (ROWS, OBS), 0)
+    lane_id = lax.broadcasted_iota(jnp.int32, (128, OBS), 0)
+    for t in range(2):
+        row_hot[t] = jnp.where(row_id == row[t:t + 1], 1.0, 0.0).astype(BF16)
+        lane_hot[t] = jnp.where(lane_id == lane[t:t + 1], 1.0, 0.0).astype(BF16)
+    copies[5].wait()
 
 
 def spread_kernel(in_ref, out_ref, tall, lines):
@@ -353,18 +363,19 @@
     flat = pltpu.VMEM((400, 128), F32)
 
     inputs = (control_flat, spectrum_flat, jnp.asarray(np.stack(two_parts(table_x.T))),
-              jnp.asarray(np.stack(two_parts(table_y))), cases)
-    sent, back, early = call(
+              jnp.asarray(np.stack(two_parts(table_y))), cases, obs_index)
+    sent, back, early, row_hot, lane_hot = call(
         first_kernel,
-        (((32, 16, 128), BF16), ((8, 128), F32), ((2 * LEV, EARLY, MEMBERS), BF16)),
+        (((32, 16, 128), BF16), ((8, 128), F32), ((2 * LEV, EARLY, MEMBERS), BF16),
+         ((2, ROWS, OBS), BF16), ((2, 128, OBS), BF16)),
         [wide, tall, lines, grid, flat, flat, pltpu.VMEM((2, GX, GX), BF16),
-         pltpu.VMEM((2, GY, GY), BF16), pltpu.SemaphoreType.DMA((5,))],
-        "synthesis", specs=range(5),
+         pltpu.VMEM((2, GY, GY), BF16), pltpu.VMEM((2, OBS), jnp.int32), pltpu.SemaphoreType.DMA((6,))],
+        "synthesis", specs=range(6),
     )(*[pltpu.with_memory_space_constraint(value, pltpu.HBM) for value in inputs])
     pieces = exchanged(sent, SPACE)
     (copies,) = call(spread_kernel, (((8, 400, 128), BF16),), [tall, flat], "spread")(pieces)
     fields = exchanged(copies, TM)
-    partial, obs = middle(early, cases, fields, obs_index, innovation, obs_sigma, qc_class)
+    partial, obs = middle(early, cases, fields, row_hot, lane_hot, obs_index, innovation, obs_sigma, qc_class)
     terms = exchanged(partial, TM)
     (summed,) = call(fold_kernel, (((32, 16, 128), BF16),), [tall], "fold")(terms)
     adjoint = exchanged(summed, SPACE)

time: 100 us -> 100 us (level)
  no operation moved by 1% of the time
where the time goes in v8:
time: 100 us; the launch traced here: 99.9 us
  blocking collectives  89.2 us (89%)
  Pallas kernels  9.9 us (10%)
    all_to_all x5, blocking collectives, exchanged(): return lax.all_to_all(value, axis, split_axis=0, concat_axis=0, tiled=True)  89.2 us
    pallas_call x5, Pallas kernels, run(): pl.pallas_call(kernel, out_shape=tuple((jax.ShapeDtypeStruct(*out) for ou...  5.59 us
    pallas_call x1, Pallas kernels, middle(): pl.pallas_call(middle_kernel, out_shape=(jax.ShapeDtypeStruct((8, 400, 12...  4.3 us

profile of v8, /device:TPU:1, one launch (start us, length us, event | category | flops | bytes accessed | tf_op | source)
XLA Modules:
  0.0 99.9 jit_solution(16430457888760568785)
XLA Ops:
  0.6 0.0 copy-start.6
  0.6 0.0 copy-start.9
  0.7 0.0 copy-start.8
  0.7 0.0 copy-start.7
  0.7 3.0 %synthesis.1 = (bf16[32,16,128]{2,1,0:T(8,128)(2,1)S(1)}, f32[8,128]{1,0:T(8,128)S(1)}, bf16[8,1280,256]{2,1,0:T(8,128)(2,1)S(1)}, bf16[2,64,2048]{2,1,0:T(8,128)(2,1)S(1)}, bf16[2,128,2048]{2,1,0:T(8,128)(2,1)S(1)}) custom-call(f32[400,128]{1,0:T(8,128)} %bitcast.11, f32[400,128]{1,0:T(8,128)} %bitcast.14, bf16[2,320,320]{2,1,0:T(8,128)(2,1)} %constant.12.clone.x_hbm, ...), custom_call_target="tpu_custom_call" | custom-call | tf_op jit(solution)/shard_map/synthesis/pallas_call | solution.py:334
  3.7 23.4 %all_to_all.25.in_ref = bf16[32,16,128]{2,1,0:T(8,128)(2,1)S(1)} all-to-all(bf16[32,16,128]{2,1,0:T(8,128)(2,1)S(1)} %get-tuple-element.14), channel_id=1, replica_groups=mesh['tm_0'=2,'tm_1'=4,'space_0'=4,'space_1'=4,'space_2'=2] {'space_0','..., dimensions={0} | all-to-all | bytes 262144 | tf_op jit(solution)/shard_map/all_to_all | solution.py:348
  27.1 0.2 spread.1
  27.3 17.2 %all_to_all.26.f_ref = bf16[8,400,128]{2,1,0:T(8,128)(2,1)S(1)} all-to-all(bf16[8,400,128]{2,1,0:T(8,128)(2,1)S(1)} %spread.1), channel_id=1, replica_groups=mesh['tm_0'=2,'tm_1'=4,'space_0'=4,'space_1'=4,'space_2'=2] {'tm_0','tm_1'}, dimensions={0} | all-to-all | bytes 1638400 | tf_op jit(solution)/shard_map/all_to_all | solution.py:348
  44.5 0.0 copy-done.6
  44.5 0.0 copy-done.9
  44.5 0.0 copy-done.8
  44.5 0.0 copy-done.7
  44.5 0.0 copy-start
  44.5 0.0 copy-start.1
  44.5 0.0 copy-start.2
  44.5 0.0 copy-start.3
  44.6 0.0 copy-start.4
  44.6 0.0 copy-start.5
  44.6 4.3 %middle.1 = (bf16[8,400,128]{2,1,0:T(8,128)(2,1)S(1)}, f32[8,128]{1,0:T(8,128)S(1)}) custom-call(bf16[8,1280,256]{2,1,0:T(8,128)(2,1)S(1)} %get-tuple-element.13.early_ref, bf16[8,1600,256]{2,1,0:T(8,128)(2,1)} %bitcast.19, bf16[8,400,128]{2,1,0:T(8,128)(2,1)S(1)} %all_to_all.26.f_ref, bf16[2,64,2048]{2,1,0:T(8,128)(2,1)S(1)} %get-tuple-element.15.row_hot, ...), custom_call_target="tpu_custom_call" | custom-call | tf_op jit(solution)/shard_map/middle/pallas_call | solution.py:162
  48.9 14.7 %all_to_all.27.in_ref = bf16[8,400,128]{2,1,0:T(8,128)(2,1)S(1)} all-to-all(bf16[8,400,128]{2,1,0:T(8,128)(2,1)S(1)} %get-tuple-element.17), channel_id=1, replica_groups=mesh['tm_0'=2,'tm_1'=4,'space_0'=4,'space_1'=4,'space_2'=2] {'tm_0','tm_1'}, dimensions={0} | all-to-all | bytes 1638400 | tf_op jit(solution)/shard_map/all_to_all | solution.py:348
  63.6 0.3 fold.1
  63.9 16.0 %all_to_all.28.in_ref = bf16[32,16,128]{2,1,0:T(8,128)(2,1)S(1)} all-to-all(bf16[32,16,128]{2,1,0:T(8,128)(2,1)S(1)} %fold.1), channel_id=1, replica_groups=mesh['tm_0'=2,'tm_1'=4,'space_0'=4,'space_1'=4,'space_2'=2] {'space_0','..., dimensions={0} | all-to-all | bytes 262144 | tf_op jit(solution)/shard_map/all_to_all | solution.py:348
  79.9 0.0 copy-done
  79.9 0.0 copy-done.1
  79.9 0.0 copy-done.2
  79.9 0.0 copy-done.3
  79.9 0.0 copy-done.4
  79.9 0.0 copy-done.5
  80.0 1.2 %analysis.1 = (f32[400,128]{1,0:T(8,128)S(1)}, f32[256,128]{1,0:T(8,128)S(1)}) custom-call(bf16[32,16,128]{2,1,0:T(8,128)(2,1)S(1)} %all_to_all.28.in_ref, f32[400,128]{1,0:T(8,128)S(1)} %bitcast.12, f32[400,128]{1,0:T(8,128)S(1)} %bitcast.15, bf16[320,320]{1,0:T(8,128)(2,1)S(1)} %copy-done.3, bf16[320,320]{1,0:T(8,128)(2,1)S(1)} %copy-done.2, ...), custom_call_target="tpu_custom_call" | custom-call | tf_op jit(solution)/shard_map/analysis/pallas_call | solution.py:334
  81.2 17.9 %all_to_all.29 = f32[256,1,128]{2,1,0:T(1,128)S(1)} all-to-all(f32[256,1,128]{2,1,0:T(1,128)S(1)} %bitcast.17), channel_id=1, replica_groups=mesh['tm_0'=2,'tm_1'=4,'space_0'=4,'space_1'=4,'space_2'=2] {'tm_0','tm_..., dimensions={0} | all-to-all | bytes 262144 | tf_op jit(solution)/shard_map/all_to_all | solution.py:348
  99.1 0.9 step.1
Async XLA Ops:
  0.6 43.9 %copy-start.6 = (s32[2,2048]{1,0:T(2,128)S(1)}, s32[2,2048]{1,0:T(2,128)}, u32[]{:S(2)}) copy-start(s32[2,2048]{1,0:T(2,128)} %idx_ref.1) | copy-start | bytes 49156
  0.6 43.9 %copy-start.9 = (s32[2,2048]{1,0:T(2,128)S(1)}, s32[2,2048]{1,0:T(2,128)}, u32[]{:S(2)}) copy-start(s32[2,2048]{1,0:T(2,128)} %qc_ref.1) | copy-start | bytes 49156
  0.7 43.8 %copy-start.8 = (f32[2,2048]{1,0:T(2,128)S(1)}, f32[2,2048]{1,0:T(2,128)}, u32[]{:S(2)}) copy-start(f32[2,2048]{1,0:T(2,128)} %sig_ref.1) | copy-start | bytes 49156
  0.7 43.8 %copy-start.7 = (f32[2,2048]{1,0:T(2,128)S(1)}, f32[2,2048]{1,0:T(2,128)}, u32[]{:S(2)}) copy-start(f32[2,2048]{1,0:T(2,128)} %inn_ref.1) | copy-start | bytes 49156
  44.5 35.4 %copy-start = (f32[1,51200]{1,0:T(1,128)S(1)}, f32[1,51200]{1,0:T(1,128)}, u32[]{:S(2)}) copy-start(f32[1,51200]{1,0:T(1,128)} %param.13) | copy-start | bytes 614404
  44.5 35.4 %copy-start.1 = (f32[51200]{0:T(1024)S(1)}, f32[51200]{0:T(1024)}, u32[]{:S(2)}) copy-start(f32[51200]{0:T(1024)} %param.14) | copy-start | bytes 614404
  44.5 35.4 %copy-start.2 = (bf16[320,320]{1,0:T(8,128)(2,1)S(1)}, bf16[320,320]{1,0:T(8,128)(2,1)}, u32[]{:S(2)}) copy-start(bf16[320,320]{1,0:T(8,128)(2,1)} %constant.15.clone.xl) | copy-start | bytes 614404
  44.5 35.4 %copy-start.3 = (bf16[320,320]{1,0:T(8,128)(2,1)S(1)}, bf16[320,320]{1,0:T(8,128)(2,1)}, u32[]{:S(2)}) copy-start(bf16[320,320]{1,0:T(8,128)(2,1)} %constant.14.clone.xh) | copy-start | bytes 614404
  44.6 35.4 %copy-start.4 = (bf16[160,160]{1,0:T(8,128)(2,1)S(1)}, bf16[160,160]{1,0:T(8,128)(2,1)}, u32[]{:S(2)}) copy-start(bf16[160,160]{1,0:T(8,128)(2,1)} %constant.17.clone.yl) | copy-start | bytes 153604
  44.6 35.4 %copy-start.5 = (bf16[160,160]{1,0:T(8,128)(2,1)S(1)}, bf16[160,160]{1,0:T(8,128)(2,1)}, u32[]{:S(2)}) copy-start(bf16[160,160]{1,0:T(8,128)(2,1)} %constant.16.clone.yh) | copy-start | bytes 153604
